TPU v7x, 512 devices: a whole 4x8x8 slice. The times are simulated.
512 devices in a mesh: req: 64 (over x, y, core), tp: 8 (over z).
Axes of the slice: x: 4, y: 8, z: 8, core: 2. Of those that a mesh axis runs over, the one named last changes fastest.
Arguments:
- queries: bfloat16 [64, 28, 4096], P('req', None, 'tp'), may hold values from -25 to 25
- tree_kv: bfloat16 [64, 28, 2048], P('req', None, 'tp'), may hold values from -4 to 4
- tree_parent: int32 [64, 28], P('req'), may hold values from -1 to 26, as said below
- accepted_path: int32 [64, 8], replicated, may hold values from -1 to 27, as said below
- cache_kv: bfloat16 [192, 256, 2048], P('req', None, 'tp'), may hold values from -6 to 6
- piece_owner: int32 [192, 2], P('req'), may hold values from -1 to 63, as said below
- cache_len: int32 [64], replicated, may hold values from 1 to 1016, as said below
- out_weight: bfloat16 [4096, 4096], P('tp', 'req'), may hold values from -0.09375 to 0.09375
Outputs:
- mixed: bfloat16 [64, 28, 4096], P('tp', None, 'req')
- cache_out: bfloat16 [192, 256, 2048], P('req', None, 'tp')
Inputs may be any that keep to these rules, and one draw needn't show every extreme that they name: tree_parent[r, 0] = -1 and 0 <= tree_parent[r, i] < i for i >= 1; tokens 1 to 7 have parent i - 1. accepted_path[r] lists, root first, the tokens on the path from token 0 to some token of request r's tree, then -1 entries; it holds 1 to 8 tokens, and 8 for some request. piece_owner[s] = (r, p) means slot s holds cache rows p * 256 to p * 256 + 255 of request r; (-1, -1) marks an unused slot. For each request r the pieces 0 to (cache_len[r] + 7) // 256 stand in exactly one slot each, and no other pieces do. cache_len[r] + 8 <= 1024.
All inputs are finite; a program needn't handle non-finite values.
Results may differ from a plain program's by a relative error of at most 0.02.
Values may be sent and summed in bfloat16 or wider, within the bound.
No kernel may reach another device: no remote copies, remote signals or barrier semaphores. Data moves between devices by JAX's collectives and lax.ppermute only.
A program may use at most 64 MiB of HBM per device.

v0:
```python
import math

import jax
import jax.numpy as jnp
from jax import lax
from jax.sharding import PartitionSpec as P

HD = 128


NEG = -1e30


def ancestors(parent):
    tree_size = parent.shape[-1]
    node_ids = lax.broadcasted_iota(jnp.int32, (tree_size, tree_size), 1)
    parent_hot = (parent[..., :, None] == node_ids).astype(jnp.float32)
    reached = jnp.minimum(parent_hot + jnp.eye(tree_size, dtype=jnp.float32), 1.0)
    for rounds in range(max(1, (tree_size - 1).bit_length())):
        reached = jnp.minimum(
            jnp.einsum("rij,rjk->rik", reached, reached, precision=lax.Precision.HIGHEST), 1.0
        )
    return reached


def shards(
    queries, tree_kv, tree_parent, accepted_path, cache_kv, piece_owner, cache_len, out_weight
):
    kvheads_local = tree_kv.shape[-1] // (2 * HD)
    heads_local = queries.shape[-1] // HD
    group_size = heads_local // kvheads_local
    tree_size = queries.shape[1]
    slot_count = cache_kv.shape[0]
    piece_rows = cache_kv.shape[1]
    depth_most = accepted_path.shape[1]
    scaling = 1.0 / math.sqrt(HD)
    every_query = lax.all_gather(queries, "req", axis=0, tiled=True)
    req_total = every_query.shape[0]
    owner_req = piece_owner[:, 0]
    owner_piece = piece_owner[:, 1]
    safe_req = jnp.maximum(owner_req, 0)
    slot_query = every_query[safe_req].reshape(slot_count, tree_size, kvheads_local, group_size, HD)
    stored = cache_kv.reshape(slot_count, piece_rows, kvheads_local, 2, HD)
    row_pos = owner_piece[:, None] * piece_rows + lax.broadcasted_iota(
        jnp.int32, (slot_count, piece_rows), 1
    )
    visible = (owner_req >= 0)[:, None] & (row_pos < cache_len[safe_req][:, None])
    wide_mask = visible[:, None, None, None, :]
    scores = (
        jnp.einsum(
            "stkgd,spkd->stkgp", slot_query, stored[:, :, :, 0], preferred_element_type=jnp.float32
        )
        * scaling
    )
    scores = jnp.where(wide_mask, scores, NEG)
    slot_peak = jnp.max(scores, -1)
    expo = jnp.where(wide_mask, jnp.exp(scores - slot_peak[..., None]), 0.0)
    slot_den = jnp.sum(expo, -1)
    weights = expo.astype(jnp.bfloat16)
    slot_num = jnp.einsum(
        "stkgp,spkd->stkgd", weights, stored[:, :, :, 1], preferred_element_type=jnp.float32
    )
    request_ids = lax.broadcasted_iota(jnp.int32, (req_total, slot_count), 0)
    member = (owner_req[None, :] == request_ids)[:, :, None, None, None]
    req_peak = jnp.max(jnp.where(member, slot_peak[None], NEG), axis=1)
    factor = jnp.where(
        member, jnp.exp(jnp.where(member, slot_peak[None] - req_peak[:, None], 0.0)), 0.0
    )
    req_den = jnp.sum(factor * slot_den[None], axis=1)
    req_num = jnp.einsum("rstkg,stkgd->rtkgd", factor, slot_num, precision=lax.Precision.HIGHEST)
    peak_table = req_peak.reshape(req_total, tree_size, heads_local)
    den_table = req_den.reshape(req_total, tree_size, heads_local)
    num_table = req_num.reshape(req_total, tree_size, heads_local * HD)
    own_index = lax.axis_index("req")
    got_peak, got_den, got_num = (
        lax.all_to_all(
            peak_table.astype(jnp.bfloat16), "req", split_axis=0, concat_axis=0, tiled=True
        ).astype(peak_table.dtype),
        lax.all_to_all(
            den_table.astype(jnp.bfloat16), "req", split_axis=0, concat_axis=0, tiled=True
        ).astype(den_table.dtype),
        lax.all_to_all(
            num_table.astype(jnp.bfloat16), "req", split_axis=0, concat_axis=0, tiled=True
        ).astype(num_table.dtype),
    )
    cache_peak = jnp.max(got_peak, axis=0)
    source_scale = jnp.exp(got_peak - cache_peak[None])
    cache_den = jnp.sum(source_scale * got_den, axis=0)
    got_rows = got_num.reshape(got_num.shape[0], tree_size, heads_local, HD)
    cache_num = jnp.sum(source_scale[..., None] * got_rows, axis=0)
    reached = ancestors(tree_parent)[0]
    home_query = queries[0].reshape(tree_size, kvheads_local, group_size, HD)
    fresh = tree_kv[0].reshape(tree_size, kvheads_local, 2, HD)
    tree_mask = reached[:, None, None, :] > 0.5
    tree_scores = (
        jnp.einsum("ikgd,jkd->ikgj", home_query, fresh[:, :, 0], preferred_element_type=jnp.float32)
        * scaling
    )
    tree_scores = jnp.where(tree_mask, tree_scores, NEG)
    tree_peak = jnp.max(tree_scores, -1)
    tree_exp = jnp.where(tree_mask, jnp.exp(tree_scores - tree_peak[..., None]), 0.0)
    tree_den = jnp.sum(tree_exp, -1).reshape(tree_size, heads_local)
    tree_num = jnp.einsum(
        "ikgj,jkd->ikgd",
        tree_exp.astype(jnp.bfloat16),
        fresh[:, :, 1],
        preferred_element_type=jnp.float32,
    )
    tree_num = tree_num.reshape(tree_size, heads_local, HD)
    tree_peak = tree_peak.reshape(tree_size, heads_local)
    total_peak = jnp.maximum(cache_peak, tree_peak)
    cache_scale = jnp.exp(cache_peak - total_peak)
    tree_scale = jnp.exp(tree_peak - total_peak)
    denom = cache_den * cache_scale + tree_den * tree_scale
    numer = cache_num * cache_scale[..., None] + tree_num * tree_scale[..., None]
    attention = (
        (numer / denom[..., None]).reshape(1, tree_size, heads_local * HD).astype(jnp.bfloat16)
    )
    piece = lax.all_gather(attention, "req", axis=0, tiled=True)
    flat_rows = piece.reshape(piece.shape[0] * piece.shape[1], piece.shape[2])
    product = jnp.dot(flat_rows, out_weight, preferred_element_type=jnp.float32)
    terms = product.reshape(piece.shape[0], piece.shape[1], out_weight.shape[1])
    mixed = lax.psum_scatter(terms.astype(jnp.bfloat16), "tp", scatter_dimension=0, tiled=True)
    own_path = lax.dynamic_index_in_dim(accepted_path, own_index, 0, keepdims=False)
    picked = tree_kv[0][jnp.maximum(own_path, 0)]
    picked = jnp.where((own_path >= 0)[:, None], picked, jnp.zeros_like(picked))
    all_rows = lax.all_gather(picked[None], "req", axis=0, tiled=True)
    counts = jnp.sum((accepted_path >= 0).astype(jnp.int32), axis=1)
    offset = row_pos - cache_len[safe_req][:, None]
    writing = (owner_req >= 0)[:, None] & (offset >= 0) & (offset < counts[safe_req][:, None])
    slot_rows = all_rows[safe_req]
    chosen = jnp.take_along_axis(slot_rows, jnp.clip(offset, 0, depth_most - 1)[:, :, None], axis=1)
    cache_out = jnp.where(writing[:, :, None], chosen, cache_kv)
    return (mixed, cache_out)


def solution(mesh):
    return jax.shard_map(
        shards,
        mesh=mesh,
        in_specs=(
            P("req", None, "tp"),
            P("req", None, "tp"),
            P("req", None),
            P(),
            P("req", None, "tp"),
            P("req", None),
            P(),
            P("tp", "req"),
        ),
        out_specs=(P("tp", None, "req"), P("req", None, "tp")),
        check_vma=False,
    )
```

profile of v0, /device:TPU:6, one launch (start us, length us, event | category | flops | bytes accessed | tf_op | source)
XLA Modules:
  0.0 330.9 jit_solution(16705288890588195445)
XLA Ops:
  7.2 0.7 all-gather.3.cloned.1.call-update
  7.9 1.2 copy.126
  9.1 0.8 slice_bitcast_fusion.4
  9.9 0.7 convert_reduce_fusion
  10.6 0.6 gather_fusion.2
  11.2 1.3 gather_fusion
  12.6 0.7 compare_bitcast_fusion
  13.3 84.2 %all-gather.3.cloned.1.call-done = bf16[64,28,512]{2,1,0:T(8,128)(2,1)} async-done(((bf16[1,28,512]{2,1,0:T(8,128)(2,1)}), bf16[64,28,512]{2,1,0:T(8,128)(2,1)}) %all-gather.3.cloned.1.call-update) | async-done | bytes 1835024 | tf_op jit(solution)/shard_map/all_gather | solution.py:37
  97.6 2.1 gather_fusion.1
  99.7 0.3 fusion.62
  100.0 0.1 copy.129
  100.2 0.2 fusion.11
  100.4 0.3 fusion.19
  100.7 0.2 select_reduce_fusion
  100.9 0.8 copy.130
  101.6 8.2 %all-to-all-start = ((bf16[64,28,4]{1,2,0:T(4,128)(2,1)}), bf16[64,28,4]{1,2,0:T(4,128)(2,1)S(1)}, u32[]{:S(2)}, u32[]{:S(2)}) async-start(bf16[64,28,4]{1,2,0:T(4,128)(2,1)} %copy.130), calls=%async_computation | async-start | bytes 131072 | tf_op jit(solution)/shard_map/all_to_all | solution.py:76
  109.8 0.1 copy.150
  109.9 0.3 multiply_reduce_fusion.1
  110.2 0.1 copy.137
  110.3 0.8 copy.151
  111.1 6.5 %all-to-all-done = bf16[64,28,4]{1,2,0:T(4,128)(2,1)S(1)} async-done(((bf16[64,28,4]{1,2,0:T(4,128)(2,1)}), bf16[64,28,4]{1,2,0:T(4,128)(2,1)S(1)}, u32[]{:S(2)}, u32[]{:S(2)}) %all-to-all-start) | async-done | bytes 14368 | tf_op jit(solution)/shard_map/all_to_all | solution.py:76
  117.6 6.6 %all-to-all-start.2 = ((bf16[64,28,4]{1,2,0:T(4,128)(2,1)}), bf16[64,28,4]{1,2,0:T(4,128)(2,1)S(1)}, u32[]{:S(2)}, u32[]{:S(2)}) async-start(bf16[64,28,4]{1,2,0:T(4,128)(2,1)} %copy.151), calls=%async_computation.2 | async-start | bytes 131072 | tf_op jit(solution)/shard_map/all_to_all | solution.py:79
  124.1 6.0 %convert_bitcast_fusion = bf16[64,28,1,4,128]{4,0,3,1,2:T(8,128)(2,1)S(1)} fusion(f32[3,28,4,128]{3,1,2,0:T(8,128)S(1)} %fusion.19, f32[64,28,4]{0,2,1:T(4,128)S(1)} %select_reduce_fusion, f32[3,28,4]{0,2,1:T(4,128)S(1)} %copy.137, pred[64,3]{0,1:T(4,128)(4,1)S(1)} %iota_compare_fusion), kind=kOutput, calls=%fused_computation.9 | convolution fusion | flops 34012160 | bytes 2037248 | tf_op jit(solution)/shard_map/rstkg,stkgd->rtkgd/dot_general | solution.py:70
  130.2 1.4 copy.161
  131.6 1.8 reshape.676
  133.4 10.6 %all-to-all-start.1 = ((bf16[64,28,512]{2,1,0:T(8,128)(2,1)}), bf16[64,28,512]{2,1,0:T(8,128)(2,1)S(1)}, u32[]{:S(2)}, u32[]{:S(2)}) async-start(bf16[64,28,512]{2,1,0:T(8,128)(2,1)} %reshape.676), calls=%async_computation.1 | async-start | bytes 4194304 | tf_op jit(solution)/shard_map/all_to_all | solution.py:82
  144.2 0.1 fusion.42
  144.3 0.1 convolution_minimum_fusion.4
  144.5 0.1 convolution_minimum_fusion.3
  144.6 0.1 convolution_minimum_fusion.2
  144.8 0.1 convolution_minimum_fusion.1
  144.9 0.2 fusion.10
  145.1 0.1 copy.142
  145.2 0.2 fusion.61
  145.4 0.2 convolution_bitcast_fusion
  145.8 0.1 copy.134
  145.9 0.1 copy.131
  146.0 0.1 copy.152
  146.1 0.2 subtract_exponential_fusion
  146.4 0.1 copy.155
  146.5 0.1 copy.149
  146.6 0.1 copy.145
  146.7 0.4 copy.135
  147.1 3.5 %mul.113 = f32[64,28,4,128]{3,2,0,1:T(4,128)} broadcast(f32[64,28,4]{2,0,1:T(8,128)S(1)} %copy.135), dimensions={0,1,2} | broadcast | bytes 3698688 | tf_op jit(solution)/shard_map/mul | solution.py:90
  150.6 5.2 %mul.114 = f32[64,28,512]{2,0,1:T(8,128)} reshape(f32[64,28,4,128]{3,2,0,1:T(4,128)} %mul.113) | data formatting | bytes 7340032 | tf_op jit(solution)/shard_map/mul | solution.py:90
  155.9 37.2 %all-to-all-done.1 = bf16[64,28,512]{2,1,0:T(8,128)(2,1)S(1)} async-done(((bf16[64,28,512]{2,1,0:T(8,128)(2,1)}), bf16[64,28,512]{2,1,0:T(8,128)(2,1)S(1)}, u32[]{:S(2)}, u32[]{:S(2)}) %all-to-all-start.1) | async-done | bytes 1835040 | tf_op jit(solution)/shard_map/all_to_all | solution.py:82
  193.0 3.6 %multiply_reduce_fusion = f32[28,512]{1,0:T(8,128)S(1)} fusion(f32[64,28,512]{2,0,1:T(8,128)} %mul.114, bf16[64,28,512]{2,1,0:T(8,128)(2,1)S(1)} %all-to-all-done.1), kind=kLoop, calls=%fused_computation.6 | loop fusion | flops 2738176 | bytes 5562368 | tf_op jit(solution)/shard_map/reduce_sum | solution.py:90
  196.7 0.1 mul.123
  196.9 0.1 fusion.30
  197.0 0.6 copy.156
  197.7 0.2 maximum_reduce_fusion
  197.9 0.6 gather_fusion.3
  198.5 0.2 compare_reduce_fusion
  198.8 37.8 %all_gather.11 = bf16[64,8,256]{2,1,0:T(8,128)(2,1)S(1)} all-gather(bf16[1,8,256]{2,1,0:T(8,128)(2,1)S(1)} %bitcast_select_fusion), channel_id=1, replica_groups=mesh['req'=64,'tp'=8] {'req'}, dimensions={0}, use_global_device_ids=true | all-gather | bytes 266240 | tf_op jit(solution)/shard_map/all_gather | solution.py:127
  236.6 0.5 gather_fusion.4
  237.2 41.2 %all-gather.5.cloned.1.call-done = bf16[64,28,512]{2,1,0:T(8,128)(2,1)} async-done(((bf16[1,28,512]{2,1,0:T(8,128)(2,1)}), bf16[64,28,512]{2,1,0:T(8,128)(2,1)}) %all-gather.5.cloned.1.call-update) | async-done | bytes 1835024 | tf_op jit(solution)/shard_map/all_gather | solution.py:119
  278.4 3.7 %fusion.2 = bf16[64,28,64]{2,0,1:T(8,128)(2,1)S(1)} fusion(bf16[64,28,512]{2,1,0:T(8,128)(2,1)} %all-gather.5.cloned.1.call-done, bf16[512,64]{0,1:T(8,128)(2,1)S(1)} %copy-done), kind=kOutput, calls=%fused_computation.10 | convolution fusion | flops 117555200 | bytes 2129920 | tf_op jit(solution)/shard_map/dot_general | solution.py:121
  282.1 0.3 copy.162
  282.4 1.1 reshape.677
  283.6 4.2 %gather_fusion.5 = bf16[768,256]{1,0:T(8,128)(2,1)S(1)} fusion(bf16[3,8,256]{2,1,0:T(8,128)(2,1)S(1)} %gather_fusion.4, s32[768]{0:T(1024)S(1)} %reshape.664), kind=kCustom, calls=%fused_computation.5 | custom fusion | bytes 792576 | tf_op jit(solution)/shard_map/jit(take_along_axis)/gather | solution.py:132
  287.8 1.0 select_select_fusion
  288.9 34.0 %reduce-scatter.4.cloned.1.call-done = bf16[8,1792]{1,0:T(8,128)(2,1)} async-done(((bf16[64,1792]{1,0:T(8,128)(2,1)}), bf16[8,1792]{1,0:T(8,128)(2,1)}) %reduce-scatter.4.cloned.1.call-update) | async-done | bytes 28688
  322.9 0.9 reshape.678
  323.7 0.6 copy.163
  (37 shorter events, 1.1 us)
Async XLA Ops:
  7.2 271.2 %copy-start = (bf16[512,64]{0,1:T(8,128)(2,1)S(1)}, bf16[512,64]{0,1:T(8,128)(2,1)}, u32[]{:S(2)}) copy-start(bf16[512,64]{0,1:T(8,128)(2,1)} %param.15) | copy-start | bytes 196612
  7.2 90.4 %all-gather.3.cloned.1.call-start = ((), (), s32[]{:S(2)}) async-start(), calls=%async_computation.4 | async-start | bytes 2129920 | tf_op jit(solution)/shard_map/all_gather | solution.py:37
  101.6 16.0 %all-to-all-start = ((bf16[64,28,4]{1,2,0:T(4,128)(2,1)}), bf16[64,28,4]{1,2,0:T(4,128)(2,1)S(1)}, u32[]{:S(2)}, u32[]{:S(2)}) async-start(bf16[64,28,4]{1,2,0:T(4,128)(2,1)} %copy.130), calls=%async_computation | async-start | bytes 131072 | tf_op jit(solution)/shard_map/all_to_all | solution.py:76
  117.6 15.8 %all-to-all-start.2 = ((bf16[64,28,4]{1,2,0:T(4,128)(2,1)}), bf16[64,28,4]{1,2,0:T(4,128)(2,1)S(1)}, u32[]{:S(2)}, u32[]{:S(2)}) async-start(bf16[64,28,4]{1,2,0:T(4,128)(2,1)} %copy.151), calls=%async_computation.2 | async-start | bytes 131072 | tf_op jit(solution)/shard_map/all_to_all | solution.py:79
  133.4 10.7 %copy-start.3 = (bf16[1,28,512]{2,1,0:T(8,128)(2,1)S(1)}, bf16[1,28,512]{2,1,0:T(8,128)(2,1)}, u32[]{:S(2)}) copy-start(bf16[1,28,512]{2,1,0:T(8,128)(2,1)} %param.8) | copy-start | bytes 86020
  133.4 10.7 %copy-start.2 = (bf16[1,28,256]{2,1,0:T(8,128)(2,1)S(1)}, bf16[1,28,256]{2,1,0:T(8,128)(2,1)}, u32[]{:S(2)}) copy-start(bf16[1,28,256]{2,1,0:T(8,128)(2,1)} %param.9) | copy-start | bytes 43012
  133.4 10.8 %copy-start.5 = (s32[1,28]{1,0:T(1,128)S(1)}, s32[1,28]{1,0:T(1,128)}, u32[]{:S(2)}) copy-start(s32[1,28]{1,0:T(1,128)} %param.10) | copy-start | bytes 340
  133.4 59.6 %all-to-all-start.1 = ((bf16[64,28,512]{2,1,0:T(8,128)(2,1)}), bf16[64,28,512]{2,1,0:T(8,128)(2,1)S(1)}, u32[]{:S(2)}, u32[]{:S(2)}) async-start(bf16[64,28,512]{2,1,0:T(8,128)(2,1)} %reshape.676), calls=%async_computation.1 | async-start | bytes 4194304 | tf_op jit(solution)/shard_map/all_to_all | solution.py:82
  144.1 134.3 %all-gather.5.cloned.1.call-start = ((), (), s32[]{:S(2)}) async-start(), calls=%async_computation.5 | async-start | bytes 2129920 | tf_op jit(solution)/shard_map/all_gather | solution.py:119
  155.9 41.9 %copy-start.4 = (s32[64,8]{0,1:T(8,128)S(1)}, s32[64,8]{0,1:T(8,128)}, u32[]{:S(2)}) copy-start(s32[64,8]{0,1:T(8,128)} %param.11) | copy-start | bytes 6148
  197.7 125.2 %reduce-scatter.4.cloned.1.call-start = ((), (), s32[]{:S(2)}) async-start(), calls=%async_computation.6 | async-start | bytes 258048
  283.5 4.3 %copy-start.1 = (bf16[3,256,256]{2,1,0:T(8,128)(2,1)S(1)}, bf16[3,256,256]{2,1,0:T(8,128)(2,1)}, u32[]{:S(2)}) copy-start(bf16[3,256,256]{2,1,0:T(8,128)(2,1)} %param.12) | copy-start | bytes 1179652
Sparse Core Ops, SparseCore 0:
  11.4 86.1 all-gather.2
  197.8 80.5 all-gather.4
  283.7 39.1 reduce-scatter.3
where the time goes:
time: 332 us; the launch traced here: 331 us
  waiting for transfers between devices  204 us (61%)
  blocking collectives  37.8 us (11%)
  local copies, waits for them, and re-layouts  29.6 us (9%)
  starting transfers between devices  25.5 us (8%)
  between operations  14.1 us (4%)
  matrix products  11.4 us (3%)
  other arithmetic  8.73 us (3%)
    all_gather x1, waiting for transfers between devices, shards(): every_query = lax.all_gather(queries, 'req', axis=0, tiled=True)  84.2 us
    all_gather x1, waiting for transfers between devices, shards(): piece = lax.all_gather(attention, 'req', axis=0, tiled=True)  41.2 us
    all_gather x1, blocking collectives, shards(): all_rows = lax.all_gather(picked[None], 'req', axis=0, tiled=True)  37.8 us
    all_to_all x1, waiting for transfers between devices, shards(): lax.all_to_all(num_table.astype(jnp.bfloat16), 'req', split_axis=0, conca...  37.2 us
    unnamed x4, waiting for transfers between devices  34.7 us
    all_to_all x1, starting transfers between devices, shards(): lax.all_to_all(num_table.astype(jnp.bfloat16), 'req', split_axis=0, conca...  10.6 us
    mul x2, local copies, waits for them, and re-layouts, shards(): cache_num = jnp.sum(source_scale[..., None] * got_rows, axis=0)  8.76 us
    all_to_all x1, starting transfers between devices, shards(): lax.all_to_all(peak_table.astype(jnp.bfloat16), 'req', split_axis=0, conc...  8.16 us
  transfers between devices with their start and end apart: 6, of which 5 were waited for; matrix products, arithmetic and copies ran while one was open for 10% of the time, Pallas kernels for 0%

commit v1 on v0

v1 whole, which is shorter than its diff:
```python
import functools
import math

import jax
import jax.numpy as jnp
from jax import lax
from jax.experimental import pallas as pl
from jax.experimental.pallas import tpu as pltpu
from jax.sharding import PartitionSpec as P

HD = 128
NEG = -1e30
TOK = 32
F32 = jnp.float32
BF16 = jnp.bfloat16


def iota(shape, dim):
    return lax.broadcasted_iota(jnp.int32, shape, dim)


def pack_body(owner, path, cache, tree, out):
    slots = cache.shape[0]
    own = lax.axis_index("req")
    for s in range(slots):
        out[0:32, s] = cache[s, :, 0:HD].reshape(32, 8, HD)
        out[32:64, s] = cache[s, :, HD : 2 * HD].reshape(32, 8, HD)
    lane = iota((8, HD), 1)
    row = iota((8, HD), 0)
    keys = jnp.full((8, HD), -1, jnp.int32)
    for s in range(slots):
        key = jnp.where(owner[s, 0] >= 0, owner[s, 0] * 4 + owner[s, 1], -1)
        keys = jnp.where(lane == s, key, keys)
    keyrow = jnp.where(row == 0, keys, 0).astype(F32)
    depth = path.shape[1]
    tokens = tree.shape[1]
    hot_col = iota((depth, tokens), 1)
    hot_row = iota((depth, tokens), 0)
    hot = jnp.zeros((depth, tokens), jnp.bool_)
    for d in range(depth):
        hot = hot | ((hot_row == d) & (hot_col == path[own, d]))
    rows = jnp.dot(hot.astype(BF16), tree[0], preferred_element_type=F32)
    zero = jnp.zeros((4, HD), F32)
    for h in range(4):
        chunk = rows[4 * (h % 2) : 4 * (h % 2) + 4, HD * (h // 2) : HD * (h // 2) + HD]
        tile = (jnp.concatenate([zero, chunk], axis=0) + keyrow).astype(BF16)
        for i in range(slots):
            out[4 * i + h, 3] = tile
    rest = keyrow.astype(BF16)
    for j in range(4 * slots, 64):
        out[j, 3] = rest


def route_body(got, out, table, table_s, sem):
    own = lax.axis_index("req")
    which = jnp.minimum(own // 4, 2)
    keys = got[:, 3, 0:1, :].astype(F32).reshape(64, HD)
    target = iota((64, 256), 1).astype(F32)
    source = iota((64, 256), 0).astype(F32)
    found = jnp.zeros((64, 256), F32)
    mine = jnp.zeros((64, 1), F32)
    for i in range(3):
        key = keys[:, i : i + 1]
        found = found + jnp.where(key == target, source * 4.0 + float(i), 0.0)
        mine = jnp.where(which == i, key, mine)
    holder = jnp.floor(jnp.maximum(mine, 0.0) * 0.25) * 4.0 + 3.0
    holder = jnp.sum(jnp.where(source == target, holder, 0.0), axis=0, keepdims=True)
    found = jnp.sum(found, axis=0, keepdims=True)
    table[...] = jnp.concatenate([found, holder], axis=0).astype(jnp.int32)
    copy = pltpu.make_async_copy(table, table_s, sem)
    copy.start()
    copy.wait()

    def step(r, carry):
        for p in range(4):
            t = table_s[0, 4 * r + p]
            out[r, p] = got[t // 4, t % 4]
        out[r, 4] = got[table_s[1, r] // 4, 3]
        return carry

    lax.fori_loop(0, 64, step, 0, unroll=4)


def closure(parent):
    n = TOK
    up = iota((n, n), 0)
    here = iota((n, n), 1)
    pad = jnp.concatenate([parent, jnp.full((1, n - parent.shape[1]), -1, jnp.int32)], axis=1)
    eye = (up == here).astype(F32)
    reach = jnp.minimum((up == pad).astype(F32) + eye, 1.0)
    for rounds in range(5):
        low = reach.astype(BF16)
        reach = jnp.minimum(jnp.dot(low, low, preferred_element_type=F32), 1.0)
    return lax.dot_general(
        reach.astype(BF16), eye.astype(BF16), (((0,), (0,)), ((), ())), preferred_element_type=F32
    )


def attend_body(lens, query, tree, parent, got, out, q_s, t_s):
    own = lax.axis_index("req")
    tokens = query.shape[1]
    length = lens[own]
    q_s[...] = jnp.zeros_like(q_s)
    t_s[...] = jnp.zeros_like(t_s)
    for g in range(4):
        q_s[g * TOK : g * TOK + tokens, :] = query[0, :, g * HD : (g + 1) * HD]
    t_s[0:tokens, :] = tree[0]
    q = q_s[...]
    scaling = 1.0 / math.sqrt(HD)
    dims = (((1,), (1,)), ((), ()))
    reached = closure(parent[...])
    tree_mask = jnp.concatenate([reached] * 4, axis=0) > 0.5
    tree_score = lax.dot_general(q, t_s[:, 0:HD], dims, preferred_element_type=F32) * scaling
    tree_score = jnp.where(tree_mask, tree_score, NEG)
    peak = jnp.max(tree_score, axis=1, keepdims=True)
    scores = []
    for p in range(4):
        key = got[0:32, p].reshape(256, HD)
        score = lax.dot_general(q, key, dims, preferred_element_type=F32) * scaling
        seen = iota((4 * TOK, 256), 1) < length - p * 256
        score = jnp.where(seen, score, NEG)
        peak = jnp.maximum(peak, jnp.max(score, axis=1, keepdims=True))
        scores.append(score)
    expo = jnp.where(tree_mask, jnp.exp(tree_score - peak), 0.0)
    denom = jnp.sum(expo, axis=1, keepdims=True)
    numer = jnp.dot(expo.astype(BF16), t_s[:, HD : 2 * HD], preferred_element_type=F32)
    for p in range(4):
        seen = iota((4 * TOK, 256), 1) < length - p * 256
        expo = jnp.where(seen, jnp.exp(scores[p] - peak), 0.0)
        denom = denom + jnp.sum(expo, axis=1, keepdims=True)
        value = got[32:64, p].reshape(256, HD)
        numer = numer + jnp.dot(expo.astype(BF16), value, preferred_element_type=F32)
    attention = (numer / denom).astype(BF16)
    for m in range(8):
        out[m] = attention


def append_body(owner, lens, path, cache, aux, out):
    slots = cache.shape[0]
    depth = path.shape[1]
    for s in range(slots):
        r = jnp.maximum(owner[s, 0], 0)
        count = jnp.int32(0)
        for d in range(depth):
            count = count + jnp.where(path[r, d] >= 0, 1, 0)
        count = jnp.where(owner[s, 0] >= 0, count, 0)
        first = lens[r] - owner[s, 1] * 256
        key = jnp.concatenate([aux[4 * s, 0, 4:8], aux[4 * s + 1, 0, 4:8]], axis=0)
        value = jnp.concatenate([aux[4 * s + 2, 0, 4:8], aux[4 * s + 3, 0, 4:8]], axis=0)
        fresh = jnp.concatenate([key, value], axis=1)
        pick = (iota((256, depth), 0) - first == iota((256, depth), 1)).astype(BF16)
        put = jnp.dot(pick, fresh, preferred_element_type=F32).astype(BF16)
        offset = iota((256, 2 * HD), 0) - first
        out[s] = jnp.where((offset >= 0) & (offset < count), put, cache[s])


def project_body(att, weight, out):
    left = jnp.concatenate([att[:, 0:TOK].reshape(256, HD), att[:, TOK : 2 * TOK].reshape(256, HD)], axis=1)
    right = jnp.concatenate(
        [att[:, 2 * TOK : 3 * TOK].reshape(256, HD), att[:, 3 * TOK : 4 * TOK].reshape(256, HD)], axis=1
    )
    low = iota((HD, HD), 1) < 64
    for c in range(8):
        x = jnp.dot(left, weight[c], preferred_element_type=F32)
        y = jnp.dot(right, weight[c], preferred_element_type=F32)
        first = x[0:128] + pltpu.roll(y[0:128], 64, 1)
        second = pltpu.roll(x[128:256], 64, 1) + y[128:256]
        out[c] = jnp.where(low, first, second).astype(BF16)


def total_body(got, out):
    acc = got[0].astype(F32)
    for k in range(1, 8):
        acc = acc + got[k].astype(F32)
    out[...] = acc.astype(BF16)


def place_body(got, out):
    tokens = out.shape[1]
    for h in range(2):
        for b in range(4):
            out[4 * h + b] = got[b * TOK : b * TOK + tokens, 64 * h : 64 * h + 64]


VM = pl.BlockSpec(memory_space=pltpu.VMEM)
SM = pl.BlockSpec(memory_space=pltpu.SMEM)


def call(body, name, specs, shape, scratch=()):
    return pl.pallas_call(
        body,
        name=name,
        in_specs=list(specs),
        out_specs=VM,
        out_shape=jax.ShapeDtypeStruct(shape, BF16),
        scratch_shapes=list(scratch),
    )


def shards(queries, tree_kv, tree_parent, accepted_path, cache_kv, piece_owner, cache_len, out_weight):
    tokens = queries.shape[1]
    to_all = functools.partial(lax.all_to_all, split_axis=0, concat_axis=0, tiled=True)
    near = [[8 * a + b for b in range(8)] for a in range(8)]
    far = [[8 * a + b for a in range(8)] for b in range(8)]
    with jax.named_scope("weight_gather"):
        half = out_weight.shape[0] // 2
        wide = jnp.concatenate([out_weight[:half], out_weight[half:]], axis=1)
        weight = to_all(jnp.broadcast_to(wide[None], (8,) + wide.shape), "req", axis_index_groups=far)
    with jax.named_scope("spread"):
        packed = call(pack_body, "pack", (SM, SM, VM, VM), (64, 4, 8, HD))(
            piece_owner, accepted_path, cache_kv, tree_kv
        )
        pieces = to_all(packed, "req")
    with jax.named_scope("route"):
        routed = call(
            route_body,
            "route",
            (VM,),
            (64, 5, 8, HD),
            [pltpu.VMEM((2, 256), jnp.int32), pltpu.SMEM((2, 256), jnp.int32), pltpu.SemaphoreType.DMA],
        )(pieces)
        home = to_all(routed, "req")
    with jax.named_scope("attend"):
        attention = call(
            attend_body,
            "attend",
            (SM, VM, VM, VM, VM),
            (8, 4 * TOK, HD),
            [pltpu.VMEM((4 * TOK, HD), BF16), pltpu.VMEM((TOK, 2 * HD), BF16)],
        )(cache_len, queries, tree_kv, tree_parent, home)
        gathered = to_all(attention, "req", axis_index_groups=near)
    with jax.named_scope("append"):
        cache_out = call(append_body, "append", (SM, SM, SM, VM, VM), cache_kv.shape)(
            piece_owner, cache_len, accepted_path, cache_kv, home[:12, 4:5]
        )
    with jax.named_scope("project"):
        partial = call(project_body, "project", (VM, VM), (8, 128, HD))(gathered, weight)
        partials = to_all(partial, "tp")
        total = call(total_body, "total", (VM,), (128, HD))(partials)
        pairs = [((8 * a + b) * 8 + c, (8 * c + b) * 8 + a) for a in range(8) for b in range(8) for c in range(8)]
        final = lax.ppermute(total, ("req", "tp"), pairs)
        mixed = call(place_body, "place", (VM,), (8, tokens, 64))(final)
    return (mixed, cache_out)


def solution(mesh):
    return jax.shard_map(
        shards,
        mesh=mesh,
        in_specs=(
            P("req", None, "tp"),
            P("req", None, "tp"),
            P("req", None),
            P(),
            P("req", None, "tp"),
            P("req", None),
            P(),
            P("tp", "req"),
        ),
        out_specs=(P("tp", None, "req"), P("req", None, "tp")),
        check_vma=False,
    )
```

time: 332 us -> 148 us (0.45)
  the two profiles are of different devices: /device:TPU:6 before, /device:TPU:70 now
where the time goes in v1:
time: 148 us; the launch traced here: 146 us
  blocking collectives  67 us (45%)
  waiting for transfers between devices  36.1 us (24%)
  Pallas kernels  18.4 us (12%)
  starting transfers between devices  16.9 us (11%)
  local copies, waits for them, and re-layouts  7.29 us (5%)
    all_to_all x1, blocking collectives, shards(): pieces = to_all(packed, 'req')  27.6 us
    all_to_all x1, blocking collectives, shards(): partials = to_all(partial, 'tp')  20.1 us
    all_to_all x1, blocking collectives, shards(): gathered = to_all(attention, 'req', axis_index_groups=near)  19.3 us
    all_to_all x1, waiting for transfers between devices, shards(): home = to_all(routed, 'req')  19.1 us
    ppermute x1, waiting for transfers between devices, shards(): final = lax.ppermute(total, ('req', 'tp'), pairs)  8.71 us
    all_to_all x1, waiting for transfers between devices, shards(): to_all(jnp.broadcast_to(wide[None], (8,) + wide.shape), 'req', axis_index...  8.32 us
    all_to_all x1, starting transfers between devices, shards(): home = to_all(routed, 'req')  7.03 us
    all_to_all x1, starting transfers between devices, shards(): to_all(jnp.broadcast_to(wide[None], (8,) + wide.shape), 'req', axis_index...  6.26 us
  transfers between devices with their start and end apart: 3, of which 3 were waited for; matrix products, arithmetic and copies ran while one was open for 1% of the time, Pallas kernels for 4%

profile of v1, /device:TPU:70, one launch (start us, length us, event | category | flops | bytes accessed | tf_op | source)
XLA Modules:
  0.0 146.5 jit_solution(6616392527774545537)
XLA Ops:
  0.6 1.3 copy.10.owner
  1.9 1.4 copy.11.path
  3.3 2.2 %pack.1 = bf16[64,4,8,128]{3,2,1,0:T(8,128)(2,1)} custom-call(s32[3,2]{1,0:T(4,128)} %copy.10.owner, s32[64,8]{1,0:T(8,128)} %copy.11.path, bf16[3,256,256]{2,1,0:T(8,128)(2,1)} %cache.3, bf16[1,28,256]{2,1,0:T(8,128)(2,1)} %tree.3), custom_call_target="tpu_custom_call" | custom-call | tf_op jit(solution)/shard_map/spread/pack/pallas_call | solution.py:210
  5.5 27.6 %all_to_all.25.got = bf16[64,4,8,128]{3,2,1,0:T(8,128)(2,1)} all-to-all(bf16[64,4,8,128]{3,2,1,0:T(8,128)(2,1)} %pack.1), channel_id=1, replica_groups=mesh['req'=64,'tp'=8] {'req'}, dimensions={0} | all-to-all | bytes 1048576 | tf_op jit(solution)/shard_map/spread/all_to_all | solution.py:213
  33.1 5.3 %route.1 = bf16[64,5,8,128]{3,2,1,0:T(8,128)(2,1)} custom-call(bf16[64,4,8,128]{3,2,1,0:T(8,128)(2,1)} %all_to_all.25.got), custom_call_target="tpu_custom_call" | custom-call | tf_op jit(solution)/shard_map/route/route/pallas_call | solution.py:215
  38.4 0.0 copy-start.2
  38.4 7.0 %all-to-all-start.1 = ((bf16[64,5,8,128]{3,2,1,0:T(8,128)(2,1)}), bf16[64,5,8,128]{3,2,1,0:T(8,128)(2,1)S(1)}, u32[]{:S(2)}, u32[]{:S(2)}) async-start(bf16[64,5,8,128]{3,2,1,0:T(8,128)(2,1)} %route.1), calls=%async_computation.1 | async-start | bytes 1310720 | tf_op jit(solution)/shard_map/route/all_to_all | solution.py:222
  45.5 0.0 copy-done.2
  45.5 0.1 copy.12
  45.6 19.1 %all-to-all-done.1.got = bf16[64,5,8,128]{3,2,1,0:T(8,128)(2,1)S(1)} async-done(((bf16[64,5,8,128]{3,2,1,0:T(8,128)(2,1)}), bf16[64,5,8,128]{3,2,1,0:T(8,128)(2,1)S(1)}, u32[]{:S(2)}, u32[]{:S(2)}) %all-to-all-start.1) | async-done | bytes 655392 | tf_op jit(solution)/shard_map/route/all_to_all | solution.py:222
  64.7 0.0 copy-start
  64.7 0.9 broadcast_in_dim.2
  65.7 0.1 copy-done
  65.8 6.3 %all-to-all-start.3 = ((bf16[8,256,128]{2,1,0:T(8,128)(2,1)}), bf16[8,256,128]{2,1,0:T(8,128)(2,1)S(1)}, u32[]{:S(2)}, u32[]{:S(2)}) async-start(bf16[8,256,128]{2,1,0:T(8,128)(2,1)} %broadcast_in_dim.2), calls=%async_computation.3 | async-start | bytes 1048576 | tf_op jit(solution)/shard_map/weight_gather/all_to_all | solution.py:208
  72.0 3.0 %attend.1 = bf16[8,128,128]{2,1,0:T(8,128)(2,1)} custom-call(s32[64]{0:T(128)} %lens.3, bf16[1,28,512]{2,1,0:T(8,128)(2,1)} %query.1, bf16[1,28,256]{2,1,0:T(8,128)(2,1)} %tree.3, s32[1,28]{1,0:T(1,128)} %parent.1, bf16[64,5,8,128]{3,2,1,0:T(8,128)(2,1)} %copy-done), custom_call_target="tpu_custom_call" | custom-call | tf_op jit(solution)/shard_map/attend/attend/pallas_call | solution.py:224
  75.1 8.3 %all-to-all-done.3.weight = bf16[8,256,128]{2,1,0:T(8,128)(2,1)S(1)} async-done(((bf16[8,256,128]{2,1,0:T(8,128)(2,1)}), bf16[8,256,128]{2,1,0:T(8,128)(2,1)S(1)}, u32[]{:S(2)}, u32[]{:S(2)}) %all-to-all-start.3) | async-done | bytes 524320 | tf_op jit(solution)/shard_map/weight_gather/all_to_all | solution.py:208
  83.4 0.0 copy-start.1
  83.4 19.3 %all_to_all.26.att = bf16[8,128,128]{2,1,0:T(8,128)(2,1)} all-to-all(bf16[8,128,128]{2,1,0:T(8,128)(2,1)} %attend.1), channel_id=1, replica_groups={{0,8,16,24,32,40,48,56},{64,72,80,88,96,104,112,120},{128,136,144,152,1..., dimensions={0} | all-to-all | bytes 524288 | tf_op jit(solution)/shard_map/attend/all_to_all | solution.py:231
  102.7 0.0 copy-done.1
  102.7 2.6 %project.1 = bf16[8,128,128]{2,1,0:T(8,128)(2,1)} custom-call(bf16[8,128,128]{2,1,0:T(8,128)(2,1)} %all_to_all.26.att, bf16[8,256,128]{2,1,0:T(8,128)(2,1)} %copy-done.1), custom_call_target="tpu_custom_call" | custom-call | tf_op jit(solution)/shard_map/project/project/pallas_call | solution.py:237
  105.3 20.1 %all_to_all.27.got = bf16[8,128,128]{2,1,0:T(8,128)(2,1)} all-to-all(bf16[8,128,128]{2,1,0:T(8,128)(2,1)} %project.1), channel_id=1, replica_groups=mesh['req'=64,'tp'=8] {'tp'}, dimensions={0} | all-to-all | bytes 524288 | tf_op jit(solution)/shard_map/project/all_to_all | solution.py:238
  125.4 1.6 %total.1 = bf16[128,128]{1,0:T(8,128)(2,1)} custom-call(bf16[8,128,128]{2,1,0:T(8,128)(2,1)} %all_to_all.27.got), custom_call_target="tpu_custom_call" | custom-call | tf_op jit(solution)/shard_map/project/total/pallas_call | solution.py:239
  127.0 3.6 %collective-permute-start = (bf16[128,128]{1,0:T(8,128)(2,1)}, bf16[128,128]{1,0:T(8,128)(2,1)S(1)}, u32[]{:S(2)}, u32[]{:S(2)}) collective-permute-start(bf16[128,128]{1,0:T(8,128)(2,1)} %total.1), channel_id=1, source_target_pairs={{0,0},{1,64},{2,128},{3,192},{4,256},{5,320},{6,384},{7,448},{8,8}... | collective-permute-start | bytes 98312 | tf_op jit(solution)/shard_map/project/ppermute | solution.py:241
  130.6 1.3 slice.12.aux
  132.0 2.2 %append.1 = bf16[3,256,256]{2,1,0:T(8,128)(2,1)} custom-call(s32[3,2]{1,0:T(4,128)} %copy.10.owner, s32[64]{0:T(128)} %lens.3, s32[64,8]{1,0:T(8,128)} %copy.11.path, bf16[3,256,256]{2,1,0:T(8,128)(2,1)} %cache.3, bf16[12,1,8,128]{3,2,1,0:T(8,128)(2,1)} %slice.12.aux), custom_call_target="tpu_custom_call" | custom-call | tf_op jit(solution)/shard_map/append/append/pallas_call | solution.py:233
  134.2 8.7 %collective-permute-done.got = bf16[128,128]{1,0:T(8,128)(2,1)S(1)} collective-permute-done((bf16[128,128]{1,0:T(8,128)(2,1)}, bf16[128,128]{1,0:T(8,128)(2,1)S(1)}, u32[]{:S(2)}, u32[]{:S(2)}) %collective-permute-start) | collective-permute-done | bytes 32800 | tf_op jit(solution)/shard_map/project/ppermute | solution.py:241
  142.9 0.0 copy-start.3
  142.9 0.6 copy-done.3
  143.5 1.5 place.1
  145.0 1.5 %copy.15 = bf16[8,28,64]{2,0,1:T(8,128)(2,1)} copy(bf16[8,28,64]{2,1,0:T(8,128)(2,1)} %place.1) | data formatting | bytes 57344
  (2 shorter events, 0.0 us)
Async XLA Ops:
  38.4 7.1 %copy-start.2 = (bf16[512,64]{0,1:T(8,128)(2,1)S(1)}, bf16[512,64]{0,1:T(8,128)(2,1)}, u32[]{:S(2)}) copy-start(bf16[512,64]{0,1:T(8,128)(2,1)} %param.15) | copy-start | bytes 196612
  38.4 26.3 %all-to-all-start.1 = ((bf16[64,5,8,128]{3,2,1,0:T(8,128)(2,1)}), bf16[64,5,8,128]{3,2,1,0:T(8,128)(2,1)S(1)}, u32[]{:S(2)}, u32[]{:S(2)}) async-start(bf16[64,5,8,128]{3,2,1,0:T(8,128)(2,1)} %route.1), calls=%async_computation.1 | async-start | bytes 1310720 | tf_op jit(solution)/shard_map/route/all_to_all | solution.py:222
  64.7 1.0 copy-start
  65.8 17.6 %all-to-all-start.3 = ((bf16[8,256,128]{2,1,0:T(8,128)(2,1)}), bf16[8,256,128]{2,1,0:T(8,128)(2,1)S(1)}, u32[]{:S(2)}, u32[]{:S(2)}) async-start(bf16[8,256,128]{2,1,0:T(8,128)(2,1)} %broadcast_in_dim.2), calls=%async_computation.3 | async-start | bytes 1048576 | tf_op jit(solution)/shard_map/weight_gather/all_to_all | solution.py:208
  83.4 19.3 %copy-start.1 = (bf16[8,256,128]{2,1,0:T(8,128)(2,1)}, bf16[8,256,128]{2,1,0:T(8,128)(2,1)S(1)}, u32[]{:S(2)}) copy-start(bf16[8,256,128]{2,1,0:T(8,128)(2,1)S(1)} %all-to-all-done.3.weight) | copy-start | bytes 1572868
  127.0 15.9 %collective-permute-start = (bf16[128,128]{1,0:T(8,128)(2,1)}, bf16[128,128]{1,0:T(8,128)(2,1)S(1)}, u32[]{:S(2)}, u32[]{:S(2)}) collective-permute-start(bf16[128,128]{1,0:T(8,128)(2,1)} %total.1), channel_id=1, source_target_pairs={{0,0},{1,64},{2,128},{3,192},{4,256},{5,320},{6,384},{7,448},{8,8}... | collective-permute-start | bytes 98312 | tf_op jit(solution)/shard_map/project/ppermute | solution.py:241
  142.9 0.6 copy-start.3

commit v2 on v1

v2 whole, which is shorter than its diff:
```python
import functools
import math

import jax
import jax.numpy as jnp
from jax import lax
from jax.experimental import pallas as pl
from jax.experimental.pallas import tpu as pltpu
from jax.sharding import PartitionSpec as P

HD = 128
NEG = -1e30
TOKENS = 28
TOK = 32
QUERY_AT = 12
TREE_AT = 28
PARENT_AT = 36
F32 = jnp.float32
BF16 = jnp.bfloat16


def iota(shape, dim):
    return lax.broadcasted_iota(jnp.int32, shape, dim)


def pack_body(owner, path, cache, query, tree, parent, out, query_f, tree_f, aux):
    slots = cache.shape[0]
    tokens = tree.shape[1]
    depth = path.shape[0]
    own = lax.axis_index("req")
    for s in range(slots):
        out[0:32, s] = cache[s, :, 0:HD].reshape(32, 8, HD)
        out[32:64, s] = cache[s, :, HD : 2 * HD].reshape(32, 8, HD)
    query_f[...] = query[0].astype(F32)
    tree_f[...] = tree[0].astype(F32)
    keys = jnp.full((8, HD), -1, jnp.int32)
    for s in range(slots):
        key = jnp.where(owner[0, s] >= 0, owner[0, s] * 4 + owner[1, s], -1)
        keys = jnp.where(iota((8, HD), 1) == s, key, keys)
    keyrow = jnp.where(iota((8, HD), 0) == 0, keys, 0).astype(F32)
    aux[...] = jnp.broadcast_to(keyrow[None], (64, 8, HD))
    hot_col = iota((depth, tokens), 1)
    hot_row = iota((depth, tokens), 0)
    hot = jnp.zeros((depth, tokens), jnp.bool_)
    for d in range(depth):
        hot = hot | ((hot_row == d) & (hot_col == path[d, own]))
    rows = jnp.dot(hot.astype(BF16), tree[0], preferred_element_type=F32)
    for h in range(4):
        chunk = rows[4 * (h % 2) : 4 * (h % 2) + 4, HD * (h // 2) : HD * (h // 2) + HD]
        for i in range(slots):
            aux[4 * i + h, 4:8] = chunk
    for g in range(4):
        for m in range(4):
            aux[QUERY_AT + 4 * g + m, 1:8] = query_f[7 * m : 7 * m + 7, g * HD : (g + 1) * HD]
    for g in range(2):
        for m in range(4):
            aux[TREE_AT + 4 * g + m, 1:8] = tree_f[7 * m : 7 * m + 7, g * HD : (g + 1) * HD]
    aux[PARENT_AT, 1:2, 0:tokens] = parent[...].astype(F32)
    out[:, 3] = aux[...].astype(BF16)


def route_body(got, out, table, table_s, sem):
    own = lax.axis_index("req")
    which = jnp.minimum(own // 4, 2)
    keys = got[:, 3, 0:1, :].astype(F32).reshape(64, HD)
    source = iota((64, 256), 0)
    lane = iota((64, 256), 1)
    place = lane // 4
    asked = place_request(place) * 4 + lane % 4
    target = asked.astype(F32)
    found = jnp.zeros((64, 256), F32)
    mine = jnp.zeros((64, 1), F32)
    tile = (source * 4).astype(F32)
    for i in range(3):
        key = keys[:, i : i + 1]
        found = found + jnp.where(key == target, tile + float(i), 0.0)
        mine = jnp.where(which == i, key, mine)
    holder = jnp.floor(jnp.maximum(mine, 0.0) * 0.25)
    holder = jnp.sum(jnp.where(source == lane, holder, 0.0), axis=0, keepdims=True)
    home = place_request(lane[0:1]).astype(F32)
    rows = jnp.where(own < QUERY_AT, holder, home) * 4.0 + 3.0
    found = jnp.sum(found, axis=0, keepdims=True)
    table[...] = jnp.concatenate([found, rows], axis=0).astype(jnp.int32)
    copy = pltpu.make_async_copy(table, table_s, sem)
    copy.start()
    copy.wait()

    def step(r, carry):
        for p in range(4):
            t = table_s[0, 4 * r + p]
            out[r, p] = got[t >> 2, t & 3]
        out[r, 4] = got[table_s[1, r] >> 2, 3]
        return carry

    lax.fori_loop(0, 64, step, 0, unroll=8)


def place_request(place):
    return (place // 16) * 16 + (place % 2) * 8 + (place // 2) % 8


def closure(parent):
    n = TOK
    up = iota((n, n), 0).astype(F32)
    here = iota((n, n), 1).astype(F32)
    eye = (up == here).astype(F32)
    reach = jnp.minimum((up == parent).astype(F32) + eye, 1.0)
    for rounds in range(5):
        low = reach.astype(BF16)
        reach = jnp.minimum(jnp.dot(low, low, preferred_element_type=F32), 1.0)
    return lax.dot_general(
        reach.astype(BF16), eye.astype(BF16), (((0,), (0,)), ((), ())), preferred_element_type=F32
    )


def attend_body(lens, got, out, query_f, tree_f):
    length = lens[place_request(lax.axis_index("req"))]
    query_f[...] = jnp.zeros_like(query_f)
    tree_f[...] = jnp.zeros_like(tree_f)
    for g in range(4):
        for m in range(4):
            at = g * TOK + 7 * m
            query_f[at : at + 7] = got[QUERY_AT + 4 * g + m, 4].astype(F32)[1:8]
    for g in range(2):
        for m in range(4):
            tree_f[7 * m : 7 * m + 7, g * HD : (g + 1) * HD] = got[TREE_AT + 4 * g + m, 4].astype(F32)[1:8]
    parent = got[PARENT_AT, 4].astype(F32)[1:2, 0:TOK]
    q = query_f[...].astype(BF16)
    fresh = tree_f[...].astype(BF16)
    scaling = 1.0 / math.sqrt(HD)
    dims = (((1,), (1,)), ((), ()))
    reached = closure(parent)
    tree_mask = jnp.concatenate([reached] * 4, axis=0) > 0.5
    tree_score = lax.dot_general(q, fresh[:, 0:HD], dims, preferred_element_type=F32) * scaling
    tree_score = jnp.where(tree_mask, tree_score, NEG)
    peak = jnp.max(tree_score, axis=1, keepdims=True)
    scores = []
    for p in range(4):
        key = got[0:32, p].reshape(256, HD)
        score = lax.dot_general(q, key, dims, preferred_element_type=F32) * scaling
        seen = iota((4 * TOK, 256), 1) < length - p * 256
        score = jnp.where(seen, score, NEG)
        peak = jnp.maximum(peak, jnp.max(score, axis=1, keepdims=True))
        scores.append(score)
    expo = jnp.where(tree_mask, jnp.exp(tree_score - peak), 0.0)
    denom = jnp.sum(expo, axis=1, keepdims=True)
    numer = jnp.dot(expo.astype(BF16), fresh[:, HD : 2 * HD], preferred_element_type=F32)
    for p in range(4):
        seen = iota((4 * TOK, 256), 1) < length - p * 256
        expo = jnp.where(seen, jnp.exp(scores[p] - peak), 0.0)
        denom = denom + jnp.sum(expo, axis=1, keepdims=True)
        value = got[32:64, p].reshape(256, HD)
        numer = numer + jnp.dot(expo.astype(BF16), value, preferred_element_type=F32)
    attention = (numer / denom).astype(BF16)
    for m in range(8):
        out[m] = attention


def append_body(owner, lens, path, cache, got, out):
    slots = cache.shape[0]
    depth = path.shape[0]
    for s in range(slots):
        r = jnp.maximum(owner[0, s], 0)
        count = jnp.int32(0)
        for d in range(depth):
            count = count + jnp.where(path[d, r] >= 0, 1, 0)
        count = jnp.where(owner[0, s] >= 0, count, 0)
        first = lens[r] - owner[1, s] * 256
        key = jnp.concatenate([got[4 * s, 4, 4:8], got[4 * s + 1, 4, 4:8]], axis=0)
        value = jnp.concatenate([got[4 * s + 2, 4, 4:8], got[4 * s + 3, 4, 4:8]], axis=0)
        fresh = jnp.concatenate([key, value], axis=1)
        pick = (iota((256, depth), 0) - first == iota((256, depth), 1)).astype(BF16)
        put = jnp.dot(pick, fresh, preferred_element_type=F32).astype(BF16)
        offset = iota((256, 2 * HD), 0) - first
        out[s] = jnp.where((offset >= 0) & (offset < count), put, cache[s])


def project_body(att, weight, out):
    rows = 8 * TOKENS
    pick = iota((rows, 256), 1) == (iota((rows, 256), 0) % 8) * TOK + iota((rows, 256), 0) // 8
    pick = pick.astype(BF16)
    parts = [att[:, g * TOK : (g + 1) * TOK].reshape(256, HD) for g in range(4)]
    both = jnp.dot(pick, jnp.concatenate(parts, axis=1), preferred_element_type=F32).astype(BF16)
    product = lax.dot_general(
        both, weight[...].reshape(512, 512), (((1,), (1,)), ((), ())), preferred_element_type=F32
    )
    half = rows // 2
    low = iota((half, HD), 1) < 64
    for c in range(8):
        x = product[:, HD * (c // 2) : HD * (c // 2) + HD]
        if c % 2 == 0:
            block = jnp.where(low, x[0:half], pltpu.roll(x[half:rows], 64, 1))
        else:
            block = jnp.where(low, pltpu.roll(x[0:half], 64, 1), x[half:rows])
        out[c] = block.astype(BF16)


def total_body(got, out):
    acc = got[0].astype(F32)
    for k in range(1, 8):
        acc = acc + got[k].astype(F32)
    out[...] = acc.astype(BF16)


def place_body(got, out):
    half = TOKENS // 2
    out[0:half] = got[:, 0:64].reshape(half, 8, 64)
    out[half:TOKENS] = got[:, 64:128].reshape(half, 8, 64)


VM = pl.BlockSpec(memory_space=pltpu.VMEM)
SM = pl.BlockSpec(memory_space=pltpu.SMEM)


def near(x):
    return pltpu.with_memory_space_constraint(x, pltpu.VMEM)


def call(body, name, specs, out, scratch=()):
    return pl.pallas_call(
        body, name=name, in_specs=list(specs), out_specs=VM, out_shape=out, scratch_shapes=list(scratch)
    )


def shards(queries, tree_kv, tree_parent, accepted_path, cache_kv, piece_owner, cache_len, out_weight):
    tokens = queries.shape[1]
    to_all = functools.partial(lax.all_to_all, split_axis=0, concat_axis=0, tiled=True)
    spot = [[16 * (a // 2) + 2 * b + a % 2 for b in range(8)] for a in range(8)]
    same_group = spot
    same_row = [[spot[a][b] for a in range(8)] for b in range(8)]
    owner = piece_owner.T
    path = accepted_path.T
    with jax.named_scope("weight_gather"):
        columns = out_weight.T
        weight = to_all(jnp.broadcast_to(columns[None], (8,) + columns.shape), "req", axis_index_groups=same_row)
    with jax.named_scope("spread"):
        packed = call(
            pack_body,
            "pack",
            (SM, SM, VM, VM, VM, VM),
            pltpu.VMEM((64, 4, 8, HD), BF16),
            [pltpu.VMEM((tokens, 4 * HD), F32), pltpu.VMEM((tokens, 2 * HD), F32), pltpu.VMEM((64, 8, HD), F32)],
        )(owner, path, cache_kv, queries, tree_kv, tree_parent)
        packed, weight = lax.optimization_barrier((packed, weight))
        pieces = to_all(packed, "req")
    with jax.named_scope("route"):
        routed = call(
            route_body,
            "route",
            (VM,),
            pltpu.VMEM((64, 5, 8, HD), BF16),
            [pltpu.VMEM((2, 256), jnp.int32), pltpu.SMEM((2, 256), jnp.int32), pltpu.SemaphoreType.DMA],
        )(near(pieces))
        home = near(to_all(routed, "req"))
    with jax.named_scope("attend"):
        attention = call(
            attend_body,
            "attend",
            (SM, VM),
            pltpu.VMEM((8, 4 * TOK, HD), BF16),
            [pltpu.VMEM((4 * TOK, HD), F32), pltpu.VMEM((TOK, 2 * HD), F32)],
        )(cache_len, home)
        gathered = to_all(attention, "req", axis_index_groups=same_group)
    with jax.named_scope("append"):
        cache_out = call(
            append_body, "append", (SM, SM, SM, VM, VM), jax.ShapeDtypeStruct(cache_kv.shape, BF16)
        )(owner, cache_len, path, cache_kv, home)
    with jax.named_scope("project"):
        partial = call(project_body, "project", (VM, VM), pltpu.VMEM((8, 4 * TOKENS, HD), BF16))(
            near(gathered), near(weight)
        )
        partials = to_all(partial, "tp")
        total = call(total_body, "total", (VM,), pltpu.VMEM((4 * TOKENS, HD), BF16))(near(partials))
        pairs = [(spot[a][b] * 8 + c, spot[c][b] * 8 + a) for a in range(8) for b in range(8) for c in range(8)]
        final = lax.ppermute(total, ("req", "tp"), pairs)
        mixed = call(place_body, "place", (VM,), jax.ShapeDtypeStruct((TOKENS, 8, 64), BF16))(near(final))
    return (mixed.transpose(1, 0, 2), cache_out)


def solution(mesh):
    return jax.shard_map(
        shards,
        mesh=mesh,
        in_specs=(
            P("req", None, "tp"),
            P("req", None, "tp"),
            P("req", None),
            P(),
            P("req", None, "tp"),
            P("req", None),
            P(),
            P("tp", "req"),
        ),
        out_specs=(P("tp", None, "req"), P("req", None, "tp")),
        check_vma=False,
    )
```

time: 148 us -> 122 us (0.82)
  the two profiles are of different devices: /device:TPU:70 before, /device:TPU:6 now
where the time goes in v2:
time: 122 us; the launch traced here: 121 us
  blocking collectives  85.6 us (70%)
  waiting for transfers between devices  12.6 us (10%)
  starting transfers between devices  11.6 us (10%)
  Pallas kernels  8.31 us (7%)
  local copies, waits for them, and re-layouts  1.67 us (1%)
    all_to_all x1, blocking collectives, shards(): home = near(to_all(routed, 'req'))  26 us
    all_to_all x1, blocking collectives, shards(): pieces = to_all(packed, 'req')  22.6 us
    all_to_all x1, blocking collectives, shards(): partials = to_all(partial, 'tp')  21.5 us
    all_to_all x1, blocking collectives, shards(): gathered = to_all(attention, 'req', axis_index_groups=same_group)  15.6 us
    all_to_all x1, starting transfers between devices, shards(): to_all(jnp.broadcast_to(columns[None], (8,) + columns.shape), 'req', axis...  9.28 us
    all_to_all x1, waiting for transfers between devices, shards(): to_all(jnp.broadcast_to(columns[None], (8,) + columns.shape), 'req', axis...  7 us
    ppermute x1, waiting for transfers between devices, shards(): final = lax.ppermute(total, ('req', 'tp'), pairs)  5.6 us
  transfers between devices with their start and end apart: 2, of which 2 were waited for; matrix products, arithmetic and copies ran while one was open for 0% of the time, Pallas kernels for 3%

profile of v2, /device:TPU:6, one launch (start us, length us, event | category | flops | bytes accessed | tf_op | source)
XLA Modules:
  0.0 120.5 jit_solution(16727801018236421331)
XLA Ops:
  0.6 1.7 %broadcast_in_dim.2 = bf16[8,64,512]{2,1,0:T(8,128)(2,1)} broadcast(bf16[64,512]{1,0:T(8,128)(2,1)} %bitcast.4), dimensions={1,2} | broadcast | bytes 589824 | tf_op jit(solution)/shard_map/weight_gather/broadcast_in_dim | solution.py:235
  2.3 9.3 %all-to-all-start = ((bf16[8,64,512]{2,1,0:T(8,128)(2,1)}), bf16[8,64,512]{2,1,0:T(8,128)(2,1)S(1)}, u32[]{:S(2)}, u32[]{:S(2)}) async-start(bf16[8,64,512]{2,1,0:T(8,128)(2,1)} %broadcast_in_dim.2), calls=%async_computation | async-start | bytes 1048576 | tf_op jit(solution)/shard_map/weight_gather/all_to_all | solution.py:235
  11.6 1.3 %pack.1 = bf16[64,4,8,128]{3,2,1,0:T(8,128)(2,1)S(1)} custom-call(s32[2,3]{1,0:T(2,128)} %bitcast.8, s32[8,64]{1,0:T(8,128)} %bitcast.6, bf16[3,256,256]{2,1,0:T(8,128)(2,1)} %cache.3, bf16[1,28,512]{2,1,0:T(8,128)(2,1)} %query.1, bf16[1,28,256]{2,1,0:T(8,128)(2,1)} %tree.1, s32[1,28]{1,0:T(1,128)} %parent.1), custom_call_target="tpu_custom_call" | custom-call | tf_op jit(solution)/shard_map/spread/pack/pallas_call | solution.py:237
  12.8 7.0 %all-to-all-done.weight = bf16[8,64,512]{2,1,0:T(8,128)(2,1)S(1)} async-done(((bf16[8,64,512]{2,1,0:T(8,128)(2,1)}), bf16[8,64,512]{2,1,0:T(8,128)(2,1)S(1)}, u32[]{:S(2)}, u32[]{:S(2)}) %all-to-all-start) | async-done | bytes 524320 | tf_op jit(solution)/shard_map/weight_gather/all_to_all | solution.py:235
  19.8 22.6 %all_to_all.25.got = bf16[64,4,8,128]{3,2,1,0:T(8,128)(2,1)S(1)} all-to-all(bf16[64,4,8,128]{3,2,1,0:T(8,128)(2,1)S(1)} %pack.1), channel_id=1, replica_groups=mesh['req'=64,'tp'=8] {'req'}, dimensions={0} | all-to-all | bytes 1048576 | tf_op jit(solution)/shard_map/spread/all_to_all | solution.py:245
  42.4 1.9 %route.1 = bf16[64,5,8,128]{3,2,1,0:T(8,128)(2,1)S(1)} custom-call(bf16[64,4,8,128]{3,2,1,0:T(8,128)(2,1)S(1)} %all_to_all.25.got), custom_call_target="tpu_custom_call" | custom-call | tf_op jit(solution)/shard_map/route/route/pallas_call | solution.py:247
  44.4 26.0 %all_to_all.26.got = bf16[64,5,8,128]{3,2,1,0:T(8,128)(2,1)S(1)} all-to-all(bf16[64,5,8,128]{3,2,1,0:T(8,128)(2,1)S(1)} %route.1), channel_id=1, replica_groups=mesh['req'=64,'tp'=8] {'req'}, dimensions={0} | all-to-all | bytes 1310720 | tf_op jit(solution)/shard_map/route/all_to_all | solution.py:254
  70.3 1.8 %attend.1 = bf16[8,128,128]{2,1,0:T(8,128)(2,1)S(1)} custom-call(s32[64]{0:T(128)} %lens.3, bf16[64,5,8,128]{3,2,1,0:T(8,128)(2,1)S(1)} %all_to_all.26.got), custom_call_target="tpu_custom_call" | custom-call | tf_op jit(solution)/shard_map/attend/attend/pallas_call | solution.py:256
  72.2 15.6 %all_to_all.27.att = bf16[8,128,128]{2,1,0:T(8,128)(2,1)S(1)} all-to-all(bf16[8,128,128]{2,1,0:T(8,128)(2,1)S(1)} %attend.1), channel_id=1, replica_groups={{0,16,32,48,64,80,96,112},{8,24,40,56,72,88,104,120},{128,144,160,176,1..., dimensions={0} | all-to-all | bytes 524288 | tf_op jit(solution)/shard_map/attend/all_to_all | solution.py:263
  87.8 0.5 project.1
  88.3 21.5 %all_to_all.28.got = bf16[8,112,128]{2,1,0:T(8,128)(2,1)S(1)} all-to-all(bf16[8,112,128]{2,1,0:T(8,128)(2,1)S(1)} %project.1), channel_id=1, replica_groups=mesh['req'=64,'tp'=8] {'tp'}, dimensions={0} | all-to-all | bytes 458752 | tf_op jit(solution)/shard_map/project/all_to_all | solution.py:272
  109.8 2.3 %collective-permute-start = (bf16[112,128]{1,0:T(8,128)(2,1)S(1)}, bf16[112,128]{1,0:T(8,128)(2,1)S(1)}, u32[]{:S(2)}, u32[]{:S(2)}) collective-permute-start(bf16[112,128]{1,0:T(8,128)(2,1)S(1)} %total.1), channel_id=1, source_target_pairs={{0,0},{1,8},{2,128},{3,136},{4,256},{5,264},{6,384},{7,392},{16,16... | collective-permute-start | bytes 86024 | tf_op jit(solution)/shard_map/project/ppermute | solution.py:275
  112.2 2.0 %append.1 = bf16[3,256,256]{2,1,0:T(8,128)(2,1)} custom-call(s32[2,3]{1,0:T(2,128)} %bitcast.9, s32[64]{0:T(128)} %lens.3, s32[8,64]{1,0:T(8,128)} %bitcast.7, bf16[3,256,256]{2,1,0:T(8,128)(2,1)} %cache.3, bf16[64,5,8,128]{3,2,1,0:T(8,128)(2,1)S(1)} %all_to_all.26.got), custom_call_target="tpu_custom_call" | custom-call | tf_op jit(solution)/shard_map/append/append/pallas_call | solution.py:265
  114.2 5.6 %collective-permute-done.got = bf16[112,128]{1,0:T(8,128)(2,1)S(1)} collective-permute-done((bf16[112,128]{1,0:T(8,128)(2,1)S(1)}, bf16[112,128]{1,0:T(8,128)(2,1)S(1)}, u32[]{:S(2)}, u32[]{:S(2)}) %collective-permute-start) | collective-permute-done | bytes 28704 | tf_op jit(solution)/shard_map/project/ppermute | solution.py:275
  119.8 0.7 place.1
  (1 shorter events, 0.0 us)
Async XLA Ops:
  2.3 17.5 %all-to-all-start = ((bf16[8,64,512]{2,1,0:T(8,128)(2,1)}), bf16[8,64,512]{2,1,0:T(8,128)(2,1)S(1)}, u32[]{:S(2)}, u32[]{:S(2)}) async-start(bf16[8,64,512]{2,1,0:T(8,128)(2,1)} %broadcast_in_dim.2), calls=%async_computation | async-start | bytes 1048576 | tf_op jit(solution)/shard_map/weight_gather/all_to_all | solution.py:235
  109.8 10.0 %collective-permute-start = (bf16[112,128]{1,0:T(8,128)(2,1)S(1)}, bf16[112,128]{1,0:T(8,128)(2,1)S(1)}, u32[]{:S(2)}, u32[]{:S(2)}) collective-permute-start(bf16[112,128]{1,0:T(8,128)(2,1)S(1)} %total.1), channel_id=1, source_target_pairs={{0,0},{1,8},{2,128},{3,136},{4,256},{5,264},{6,384},{7,392},{16,16... | collective-permute-start | bytes 86024 | tf_op jit(solution)/shard_map/project/ppermute | solution.py:275

commit v3 on v2

--- a/solution.py
+++ b/solution.py
@@ -15,6 +15,7 @@
 QUERY_AT = 12
 TREE_AT = 28
 PARENT_AT = 36
+ORDER = (0, 4, 1, 5, 3, 7, 2, 6)
 F32 = jnp.float32
 BF16 = jnp.bfloat16
 
@@ -96,7 +97,7 @@
 
 
 def place_request(place):
-    return (place // 16) * 16 + (place % 2) * 8 + (place // 2) % 8
+    return (place % 2) * 32 + (place // 16) * 8 + (place // 2) % 8
 
 
 def closure(parent):
@@ -175,24 +176,26 @@
         out[s] = jnp.where((offset >= 0) & (offset < count), put, cache[s])
 
 
-def project_body(att, weight, out):
+def project_body(att, first_weight, last_weight, out):
     rows = 8 * TOKENS
     pick = iota((rows, 256), 1) == (iota((rows, 256), 0) % 8) * TOK + iota((rows, 256), 0) // 8
     pick = pick.astype(BF16)
     parts = [att[:, g * TOK : (g + 1) * TOK].reshape(256, HD) for g in range(4)]
     both = jnp.dot(pick, jnp.concatenate(parts, axis=1), preferred_element_type=F32).astype(BF16)
-    product = lax.dot_general(
-        both, weight[...].reshape(512, 512), (((1,), (1,)), ((), ())), preferred_element_type=F32
-    )
+    own = lax.axis_index("req")
+    mine = (own % 2) * 4 + own // 16
     half = rows // 2
     low = iota((half, HD), 1) < 64
-    for c in range(8):
-        x = product[:, HD * (c // 2) : HD * (c // 2) + HD]
-        if c % 2 == 0:
-            block = jnp.where(low, x[0:half], pltpu.roll(x[half:rows], 64, 1))
-        else:
-            block = jnp.where(low, pltpu.roll(x[0:half], 64, 1), x[half:rows])
-        out[c] = block.astype(BF16)
+    dims = (((1,), (1,)), ((), ()))
+    for part, weight in enumerate((first_weight, last_weight)):
+        product = lax.dot_general(both, weight[...].reshape(256, 512), dims, preferred_element_type=F32)
+        for i in range(4):
+            x = product[:, HD * (i // 2) : HD * (i // 2) + HD]
+            if i % 2 == 0:
+                block = jnp.where(low, x[0:half], pltpu.roll(x[half:rows], 64, 1))
+            else:
+                block = jnp.where(low, pltpu.roll(x[0:half], 64, 1), x[half:rows])
+            out[mine ^ ORDER[4 * part + i]] = block.astype(BF16)
 
 
 def total_body(got, out):
@@ -225,14 +228,16 @@
 def shards(queries, tree_kv, tree_parent, accepted_path, cache_kv, piece_owner, cache_len, out_weight):
     tokens = queries.shape[1]
     to_all = functools.partial(lax.all_to_all, split_axis=0, concat_axis=0, tiled=True)
-    spot = [[16 * (a // 2) + 2 * b + a % 2 for b in range(8)] for a in range(8)]
-    same_group = spot
-    same_row = [[spot[a][b] for a in range(8)] for b in range(8)]
+    spot = [[16 * (a % 4) + 2 * b + a // 4 for b in range(8)] for a in range(8)]
+
+    def swap(x, flip):
+        return lax.ppermute(x, "req", [(spot[a][b], spot[a ^ flip][b]) for a in range(8) for b in range(8)])
+
     owner = piece_owner.T
     path = accepted_path.T
     with jax.named_scope("weight_gather"):
-        columns = out_weight.T
-        weight = to_all(jnp.broadcast_to(columns[None], (8,) + columns.shape), "req", axis_index_groups=same_row)
+        one = out_weight.T[None]
+        other = swap(one, 4)
     with jax.named_scope("spread"):
         packed = call(
             pack_body,
@@ -241,8 +246,11 @@
             pltpu.VMEM((64, 4, 8, HD), BF16),
             [pltpu.VMEM((tokens, 4 * HD), F32), pltpu.VMEM((tokens, 2 * HD), F32), pltpu.VMEM((64, 8, HD), F32)],
         )(owner, path, cache_kv, queries, tree_kv, tree_parent)
-        packed, weight = lax.optimization_barrier((packed, weight))
         pieces = to_all(packed, "req")
+        pieces, other = lax.optimization_barrier((pieces, other))
+    with jax.named_scope("weight_gather"):
+        pair = jnp.concatenate([one, other])
+        other_pair = swap(pair, 1)
     with jax.named_scope("route"):
         routed = call(
             route_body,
@@ -251,7 +259,12 @@
             pltpu.VMEM((64, 5, 8, HD), BF16),
             [pltpu.VMEM((2, 256), jnp.int32), pltpu.SMEM((2, 256), jnp.int32), pltpu.SemaphoreType.DMA],
         )(near(pieces))
-        home = near(to_all(routed, "req"))
+        home = to_all(routed, "req")
+        home, other_pair = lax.optimization_barrier((home, other_pair))
+        home = near(home)
+    with jax.named_scope("weight_gather"):
+        first_weight = jnp.concatenate([pair, other_pair])
+        last_weight = swap(first_weight, 3)
     with jax.named_scope("attend"):
         attention = call(
             attend_body,
@@ -260,14 +273,15 @@
             pltpu.VMEM((8, 4 * TOK, HD), BF16),
             [pltpu.VMEM((4 * TOK, HD), F32), pltpu.VMEM((TOK, 2 * HD), F32)],
         )(cache_len, home)
-        gathered = to_all(attention, "req", axis_index_groups=same_group)
+        gathered = to_all(attention, "req", axis_index_groups=spot)
+        gathered, last_weight = lax.optimization_barrier((gathered, last_weight))
     with jax.named_scope("append"):
         cache_out = call(
             append_body, "append", (SM, SM, SM, VM, VM), jax.ShapeDtypeStruct(cache_kv.shape, BF16)
         )(owner, cache_len, path, cache_kv, home)
     with jax.named_scope("project"):
-        partial = call(project_body, "project", (VM, VM), pltpu.VMEM((8, 4 * TOKENS, HD), BF16))(
-            near(gathered), near(weight)
+        partial = call(project_body, "project", (VM, VM, VM), pltpu.VMEM((8, 4 * TOKENS, HD), BF16))(
+            near(gathered), near(first_weight), near(last_weight)
         )
         partials = to_all(partial, "tp")
         total = call(total_body, "total", (VM,), pltpu.VMEM((4 * TOKENS, HD), BF16))(near(partials))

time: 122 us -> 111 us (0.910); the launches traced: 121 us -> 111 us
  blocking collectives: 85.6 us -> 21.6 us
  waiting for transfers between devices: 12.6 us -> 46.1 us
  starting transfers between devices: 11.6 us -> 31.8 us
  Pallas kernels: 8.31 us -> 10.7 us
  local copies, waits for them, and re-layouts: 1.67 us -> 0.01 us
    all_to_all x3 -> x0, blocking collectives: 64.1 us -> none  [the longest x1 26 us: shards(): home = near(to_all(routed, 'req'))]
    ppermute x0 -> x3, waiting for transfers between devices: none -> 17 us  [swap(): lax.ppermute(x, 'req', [(spot[a][b], spot[a ^ flip][b]) for a in range(8)...]
    all_to_all x1 -> x3, waiting for transfers between devices: 7 us -> 23.3 us  [the longest x1 13.6 us: shards(): pieces = to_all(packed, 'req')]
    all_to_all x1 -> x3, starting transfers between devices: 9.28 us -> 21.3 us  [the longest x1 10.9 us: shards(): pieces = to_all(packed, 'req')]
    ppermute x0 -> x3, starting transfers between devices: none -> 8.64 us  [swap(): lax.ppermute(x, 'req', [(spot[a][b], spot[a ^ flip][b]) for a in range(8)...]
    broadcast_in_dim x1 -> x0, local copies, waits for them, and re-layouts: 1.67 us -> none  [shards(): jnp.broadcast_to(columns[None], (8,) + columns.shape)]
  transfers between devices with their start and end apart: 2 -> 7, of which waited for: 2 -> 7; matrix products, arithmetic and copies ran while one was open for 0% -> 0% of each run, Pallas kernels for 3% -> 2%
where the time goes in v3:
time: 111 us
  waiting for transfers between devices  46.1 us (42%)
  starting transfers between devices  31.8 us (29%)
  blocking collectives  21.6 us (19%)
  Pallas kernels  10.7 us (10%)
    all_to_all x1, blocking collectives, shards(): partials = to_all(partial, 'tp')  21.6 us
    ppermute x3, waiting for transfers between devices, swap(): lax.ppermute(x, 'req', [(spot[a][b], spot[a ^ flip][b]) for a in range(8)...  17 us
    all_to_all x1, waiting for transfers between devices, shards(): pieces = to_all(packed, 'req')  13.6 us
    all_to_all x1, starting transfers between devices, shards(): pieces = to_all(packed, 'req')  10.9 us
    all_to_all x1, waiting for transfers between devices, shards(): home = to_all(routed, 'req')  8.85 us
    ppermute x3, starting transfers between devices, swap(): lax.ppermute(x, 'req', [(spot[a][b], spot[a ^ flip][b]) for a in range(8)...  8.64 us
    all_to_all x1, starting transfers between devices, shards(): home = to_all(routed, 'req')  6.9 us
    ppermute x1, waiting for transfers between devices, shards(): final = lax.ppermute(total, ('req', 'tp'), pairs)  5.72 us
  transfers between devices with their start and end apart: 7, of which 7 were waited for; matrix products, arithmetic and copies ran while one was open for 0% of the time, Pallas kernels for 2%

profile of v3, /device:TPU:6, one launch (start us, length us, event | category | flops | bytes accessed | tf_op | source)
XLA Modules:
  0.0 110.9 jit_solution(1698632180884435144)
XLA Ops:
  0.6 2.0 %pack.1 = bf16[64,4,8,128]{3,2,1,0:T(8,128)(2,1)} custom-call(s32[2,3]{1,0:T(2,128)} %bitcast.12, s32[8,64]{1,0:T(8,128)} %bitcast.10, bf16[3,256,256]{2,1,0:T(8,128)(2,1)} %cache.3, bf16[1,28,512]{2,1,0:T(8,128)(2,1)} %query.1, bf16[1,28,256]{2,1,0:T(8,128)(2,1)} %tree.1, s32[1,28]{1,0:T(1,128)} %parent.1), custom_call_target="tpu_custom_call" | custom-call | tf_op jit(solution)/shard_map/spread/pack/pallas_call | solution.py:242
  2.7 0.0 copy-start
  2.7 10.9 %all-to-all-start = ((bf16[64,4,8,128]{3,2,1,0:T(8,128)(2,1)}), bf16[64,4,8,128]{3,2,1,0:T(8,128)(2,1)S(1)}, u32[]{:S(2)}, u32[]{:S(2)}) async-start(bf16[64,4,8,128]{3,2,1,0:T(8,128)(2,1)} %pack.1), calls=%async_computation | async-start | bytes 1048576 | tf_op jit(solution)/shard_map/spread/all_to_all | solution.py:249
  13.6 0.0 copy-done
  13.6 2.1 %collective-permute-start = (bf16[1,64,512]{2,1,0:T(8,128)(2,1)S(1)}, bf16[1,64,512]{2,1,0:T(8,128)(2,1)S(1)}, u32[]{:S(2)}, u32[]{:S(2)}) collective-permute-start(bf16[1,64,512]{2,1,0:T(8,128)(2,1)S(1)} %bitcast.6), channel_id=1, source_target_pairs={{0,8},{16,24},{32,40},{48,56},{64,72},{80,88},{96,104},{112,120},{... | collective-permute-start | bytes 196616 | tf_op jit(solution)/shard_map/weight_gather/ppermute | solution.py:234
  15.7 1.1 collective-permute-done
  16.8 13.6 %all-to-all-done.got = bf16[64,4,8,128]{3,2,1,0:T(8,128)(2,1)S(1)} async-done(((bf16[64,4,8,128]{3,2,1,0:T(8,128)(2,1)}), bf16[64,4,8,128]{3,2,1,0:T(8,128)(2,1)S(1)}, u32[]{:S(2)}, u32[]{:S(2)}) %all-to-all-start) | async-done | bytes 524320 | tf_op jit(solution)/shard_map/spread/all_to_all | solution.py:249
  30.3 2.8 %route.1 = bf16[64,5,8,128]{3,2,1,0:T(8,128)(2,1)} custom-call(bf16[64,4,8,128]{3,2,1,0:T(8,128)(2,1)S(1)} %all-to-all-done.got), custom_call_target="tpu_custom_call" | custom-call | tf_op jit(solution)/shard_map/route/route/pallas_call | solution.py:255
  33.1 6.9 %all-to-all-start.1 = ((bf16[64,5,8,128]{3,2,1,0:T(8,128)(2,1)}), bf16[64,5,8,128]{3,2,1,0:T(8,128)(2,1)S(1)}, u32[]{:S(2)}, u32[]{:S(2)}) async-start(bf16[64,5,8,128]{3,2,1,0:T(8,128)(2,1)} %route.1), calls=%async_computation.1 | async-start | bytes 1310720 | tf_op jit(solution)/shard_map/route/all_to_all | solution.py:262
  40.1 2.7 %collective-permute-start.1 = (bf16[2,64,512]{2,1,0:T(8,128)(2,1)S(1)}, bf16[2,64,512]{2,1,0:T(8,128)(2,1)S(1)}, u32[]{:S(2)}, u32[]{:S(2)}) collective-permute-start(bf16[2,64,512]{2,1,0:T(8,128)(2,1)S(1)} %pad_maximum_fusion.1), channel_id=1, source_target_pairs={{0,128},{16,144},{32,160},{48,176},{64,192},{80,208},{96,224},{112... | collective-permute-start | bytes 393224 | tf_op jit(solution)/shard_map/weight_gather/ppermute | solution.py:234
  42.7 7.7 %collective-permute-done.1 = bf16[2,64,512]{2,1,0:T(8,128)(2,1)S(1)} collective-permute-done((bf16[2,64,512]{2,1,0:T(8,128)(2,1)S(1)}, bf16[2,64,512]{2,1,0:T(8,128)(2,1)S(1)}, u32[]{:S(2)}, u32[]{:S(2)}) %collective-permute-start.1) | collective-permute-done | bytes 131104 | tf_op jit(solution)/shard_map/weight_gather/ppermute | solution.py:234
  50.5 8.9 %all-to-all-done.1.got = bf16[64,5,8,128]{3,2,1,0:T(8,128)(2,1)S(1)} async-done(((bf16[64,5,8,128]{3,2,1,0:T(8,128)(2,1)}), bf16[64,5,8,128]{3,2,1,0:T(8,128)(2,1)S(1)}, u32[]{:S(2)}, u32[]{:S(2)}) %all-to-all-start.1) | async-done | bytes 655392 | tf_op jit(solution)/shard_map/route/all_to_all | solution.py:262
  59.3 2.6 %attend.1 = bf16[8,128,128]{2,1,0:T(8,128)(2,1)} custom-call(s32[64]{0:T(128)} %lens.3, bf16[64,5,8,128]{3,2,1,0:T(8,128)(2,1)S(1)} %all-to-all-done.1.got), custom_call_target="tpu_custom_call" | custom-call | tf_op jit(solution)/shard_map/attend/attend/pallas_call | solution.py:269
  61.9 3.4 %all-to-all-start.2 = ((bf16[8,128,128]{2,1,0:T(8,128)(2,1)}), bf16[8,128,128]{2,1,0:T(8,128)(2,1)S(1)}, u32[]{:S(2)}, u32[]{:S(2)}) async-start(bf16[8,128,128]{2,1,0:T(8,128)(2,1)} %attend.1), calls=%async_computation.2 | async-start | bytes 524288 | tf_op jit(solution)/shard_map/attend/all_to_all | solution.py:276
  65.3 3.9 %collective-permute-start.2 = (bf16[4,64,512]{2,1,0:T(8,128)(2,1)S(1)}, bf16[4,64,512]{2,1,0:T(8,128)(2,1)S(1)}, u32[]{:S(2)}, u32[]{:S(2)}) collective-permute-start(bf16[4,64,512]{2,1,0:T(8,128)(2,1)S(1)} %pad_maximum_fusion.first_weight), channel_id=1, source_target_pairs={{0,384},{16,400},{32,416},{48,432},{64,448},{80,464},{96,480},{112... | collective-permute-start | bytes 786440 | tf_op jit(solution)/shard_map/weight_gather/ppermute | solution.py:234
  69.3 8.2 %collective-permute-done.2.last_weight = bf16[4,64,512]{2,1,0:T(8,128)(2,1)S(1)} collective-permute-done((bf16[4,64,512]{2,1,0:T(8,128)(2,1)S(1)}, bf16[4,64,512]{2,1,0:T(8,128)(2,1)S(1)}, u32[]{:S(2)}, u32[]{:S(2)}) %collective-permute-start.2) | collective-permute-done | bytes 262176 | tf_op jit(solution)/shard_map/weight_gather/ppermute | solution.py:234
  77.5 0.9 all-to-all-done.2.att
  78.4 0.5 project.1
  78.9 21.6 %all_to_all.20.got = bf16[8,112,128]{2,1,0:T(8,128)(2,1)S(1)} all-to-all(bf16[8,112,128]{2,1,0:T(8,128)(2,1)S(1)} %project.1), channel_id=1, replica_groups=mesh['req'=64,'tp'=8] {'tp'}, dimensions={0} | all-to-all | bytes 458752 | tf_op jit(solution)/shard_map/project/all_to_all | solution.py:286
  100.5 1.9 %collective-permute-start.3 = (bf16[112,128]{1,0:T(8,128)(2,1)S(1)}, bf16[112,128]{1,0:T(8,128)(2,1)S(1)}, u32[]{:S(2)}, u32[]{:S(2)}) collective-permute-start(bf16[112,128]{1,0:T(8,128)(2,1)S(1)} %total.1), channel_id=1, source_target_pairs={{0,0},{1,128},{2,256},{3,384},{4,8},{5,136},{6,264},{7,392},{16,16... | collective-permute-start | bytes 86024 | tf_op jit(solution)/shard_map/project/ppermute | solution.py:289
  102.4 2.0 %append.1 = bf16[3,256,256]{2,1,0:T(8,128)(2,1)} custom-call(s32[2,3]{1,0:T(2,128)} %bitcast.13, s32[64]{0:T(128)} %lens.3, s32[8,64]{1,0:T(8,128)} %bitcast.11, bf16[3,256,256]{2,1,0:T(8,128)(2,1)} %cache.3, bf16[64,5,8,128]{3,2,1,0:T(8,128)(2,1)S(1)} %all-to-all-done.1.got), custom_call_target="tpu_custom_call" | custom-call | tf_op jit(solution)/shard_map/append/append/pallas_call | solution.py:279
  104.5 5.7 %collective-permute-done.3.got = bf16[112,128]{1,0:T(8,128)(2,1)S(1)} collective-permute-done((bf16[112,128]{1,0:T(8,128)(2,1)S(1)}, bf16[112,128]{1,0:T(8,128)(2,1)S(1)}, u32[]{:S(2)}, u32[]{:S(2)}) %collective-permute-start.3) | collective-permute-done | bytes 28704 | tf_op jit(solution)/shard_map/project/ppermute | solution.py:289
  110.2 0.7 place.1
  (3 shorter events, 0.1 us)
Async XLA Ops:
  2.7 10.9 %copy-start = (bf16[512,64]{0,1:T(8,128)(2,1)S(1)}, bf16[512,64]{0,1:T(8,128)(2,1)}, u32[]{:S(2)}) copy-start(bf16[512,64]{0,1:T(8,128)(2,1)} %param.15) | copy-start | bytes 196612
  2.7 27.7 %all-to-all-start = ((bf16[64,4,8,128]{3,2,1,0:T(8,128)(2,1)}), bf16[64,4,8,128]{3,2,1,0:T(8,128)(2,1)S(1)}, u32[]{:S(2)}, u32[]{:S(2)}) async-start(bf16[64,4,8,128]{3,2,1,0:T(8,128)(2,1)} %pack.1), calls=%async_computation | async-start | bytes 1048576 | tf_op jit(solution)/shard_map/spread/all_to_all | solution.py:249
  13.6 3.1 %collective-permute-start = (bf16[1,64,512]{2,1,0:T(8,128)(2,1)S(1)}, bf16[1,64,512]{2,1,0:T(8,128)(2,1)S(1)}, u32[]{:S(2)}, u32[]{:S(2)}) collective-permute-start(bf16[1,64,512]{2,1,0:T(8,128)(2,1)S(1)} %bitcast.6), channel_id=1, source_target_pairs={{0,8},{16,24},{32,40},{48,56},{64,72},{80,88},{96,104},{112,120},{... | collective-permute-start | bytes 196616 | tf_op jit(solution)/shard_map/weight_gather/ppermute | solution.py:234
  33.1 26.2 %all-to-all-start.1 = ((bf16[64,5,8,128]{3,2,1,0:T(8,128)(2,1)}), bf16[64,5,8,128]{3,2,1,0:T(8,128)(2,1)S(1)}, u32[]{:S(2)}, u32[]{:S(2)}) async-start(bf16[64,5,8,128]{3,2,1,0:T(8,128)(2,1)} %route.1), calls=%async_computation.1 | async-start | bytes 1310720 | tf_op jit(solution)/shard_map/route/all_to_all | solution.py:262
  40.1 10.4 %collective-permute-start.1 = (bf16[2,64,512]{2,1,0:T(8,128)(2,1)S(1)}, bf16[2,64,512]{2,1,0:T(8,128)(2,1)S(1)}, u32[]{:S(2)}, u32[]{:S(2)}) collective-permute-start(bf16[2,64,512]{2,1,0:T(8,128)(2,1)S(1)} %pad_maximum_fusion.1), channel_id=1, source_target_pairs={{0,128},{16,144},{32,160},{48,176},{64,192},{80,208},{96,224},{112... | collective-permute-start | bytes 393224 | tf_op jit(solution)/shard_map/weight_gather/ppermute | solution.py:234
  61.9 16.5 %all-to-all-start.2 = ((bf16[8,128,128]{2,1,0:T(8,128)(2,1)}), bf16[8,128,128]{2,1,0:T(8,128)(2,1)S(1)}, u32[]{:S(2)}, u32[]{:S(2)}) async-start(bf16[8,128,128]{2,1,0:T(8,128)(2,1)} %attend.1), calls=%async_computation.2 | async-start | bytes 524288 | tf_op jit(solution)/shard_map/attend/all_to_all | solution.py:276
  65.3 12.2 %collective-permute-start.2 = (bf16[4,64,512]{2,1,0:T(8,128)(2,1)S(1)}, bf16[4,64,512]{2,1,0:T(8,128)(2,1)S(1)}, u32[]{:S(2)}, u32[]{:S(2)}) collective-permute-start(bf16[4,64,512]{2,1,0:T(8,128)(2,1)S(1)} %pad_maximum_fusion.first_weight), channel_id=1, source_target_pairs={{0,384},{16,400},{32,416},{48,432},{64,448},{80,464},{96,480},{112... | collective-permute-start | bytes 786440 | tf_op jit(solution)/shard_map/weight_gather/ppermute | solution.py:234
  100.5 9.7 %collective-permute-start.3 = (bf16[112,128]{1,0:T(8,128)(2,1)S(1)}, bf16[112,128]{1,0:T(8,128)(2,1)S(1)}, u32[]{:S(2)}, u32[]{:S(2)}) collective-permute-start(bf16[112,128]{1,0:T(8,128)(2,1)S(1)} %total.1), channel_id=1, source_target_pairs={{0,0},{1,128},{2,256},{3,384},{4,8},{5,136},{6,264},{7,392},{16,16... | collective-permute-start | bytes 86024 | tf_op jit(solution)/shard_map/project/ppermute | solution.py:289

commit v4 on v3

v4 whole, which is shorter than its diff:
```python
import functools
import math

import jax
import jax.numpy as jnp
from jax import lax
from jax.experimental import pallas as pl
from jax.experimental.pallas import tpu as pltpu
from jax.sharding import PartitionSpec as P

HD = 128
NEG = -1e30
TOKENS = 28
TOK = 32
ORDER = (0, 1, 4, 5, 3, 2, 7, 6)
F32 = jnp.float32
BF16 = jnp.bfloat16


def iota(shape, dim):
    return lax.broadcasted_iota(jnp.int32, shape, dim)


def pack_body(owner, path, cache, query, tree, parent, out, rows, aux):
    slots = cache.shape[0]
    tokens = tree.shape[1]
    depth = path.shape[0]
    own = lax.axis_index("req")
    for s in range(slots):
        out[0:32, s] = cache[s, :, 0:HD].reshape(32, 8, HD)
        out[32:64, s] = cache[s, :, HD : 2 * HD].reshape(32, 8, HD)
    keys = jnp.full((8, HD), -1, jnp.int32)
    for s in range(slots):
        key = jnp.where(owner[0, s] >= 0, owner[0, s] * 4 + owner[1, s], -1)
        keys = jnp.where(iota((8, HD), 1) == s, key, keys)
    keyrow = jnp.where(iota((8, HD), 0) == 0, keys, 0).astype(F32)
    hot_col = iota((depth, tokens), 1)
    hot_row = iota((depth, tokens), 0)
    hot = jnp.zeros((depth, tokens), jnp.bool_)
    for d in range(depth):
        hot = hot | ((hot_row == d) & (hot_col == path[d, own]))
    fresh = jnp.dot(hot.astype(BF16), tree[0], preferred_element_type=F32)
    for y in range(8):
        aux[...] = keyrow
        two = fresh[2 * (y % 4) : 2 * (y % 4) + 2, HD * (y // 4) : HD * (y // 4) + HD]
        for i in range(slots):
            aux[2 + 2 * i : 4 + 2 * i] = two
        tile = aux[...].astype(BF16)
        for x in range(4):
            for core in range(2):
                out[16 * x + 2 * y + core, 3] = tile
    rows[...] = jnp.zeros_like(rows)
    rows[0:tokens, 0 : 4 * HD] = query[0]
    rows[0:tokens, 4 * HD : 6 * HD] = tree[0]
    rows[tokens : tokens + 1, 0:tokens] = parent[...].astype(F32).astype(BF16)


def route_body(got, out, fresh, table, table_s, sem):
    own = lax.axis_index("req")
    keys = got[:, 3, 0:1, :].astype(F32).reshape(64, HD)
    source = iota((64, 256), 0)
    lane = iota((64, 256), 1)
    target = (place_request(lane // 4) * 4 + lane % 4).astype(F32)
    tile = (source * 4).astype(F32)
    diagonal = source == lane
    found = jnp.zeros((64, 256), F32)
    holders = []
    for i in range(3):
        key = keys[:, i : i + 1]
        found = found + jnp.where(key == target, tile + float(i), 0.0)
        request = jnp.floor(jnp.maximum(key, 0.0) * 0.25)
        holders.append(jnp.sum(jnp.where(diagonal, request, 0.0), axis=0, keepdims=True))
    found = jnp.minimum(jnp.sum(found, axis=0, keepdims=True), 255.0)
    table[...] = jnp.concatenate([found] + holders, axis=0).astype(jnp.int32)
    copy = pltpu.make_async_copy(table, table_s, sem)
    copy.start()
    copy.wait()

    def step(r, carry):
        for p in range(4):
            t = table_s[0, 4 * r + p]
            out[r, p] = got[t >> 2, t & 3]
        return carry

    lax.fori_loop(0, 64, step, 0, unroll=8)
    row = iota((8, HD), 0)
    for y in range(8):
        holder = (own // 16) * 16 + 2 * y + own % 2
        tiles = [got[table_s[1 + i, holder], 3].astype(F32) for i in range(3)]
        fresh[y] = jnp.where(row < 4, tiles[0], jnp.where(row < 6, tiles[1], tiles[2])).astype(BF16)


def place_request(place):
    group = (place % 2) * 4 + place // 16
    return group * 8 + (place // 2 + 4 * (group % 2) + 2) % 8


def closure(parent):
    n = TOK
    up = iota((n, n), 0).astype(F32)
    here = iota((n, n), 1).astype(F32)
    eye = (up == here).astype(F32)
    reach = jnp.minimum((up == parent).astype(F32) + eye, 1.0)
    for rounds in range(5):
        low = reach.astype(BF16)
        reach = jnp.minimum(jnp.dot(low, low, preferred_element_type=F32), 1.0)
    return lax.dot_general(
        reach.astype(BF16), eye.astype(BF16), (((0,), (0,)), ((), ())), preferred_element_type=F32
    )


def attend_body(lens, own_rows, got, fresh_rows, out):
    length = lens[place_request(lax.axis_index("req"))]
    q = jnp.concatenate([own_rows[:, g * HD : (g + 1) * HD] for g in range(4)], axis=0)
    fresh = own_rows[:, 4 * HD : 6 * HD]
    parent = own_rows[TOKENS : TOKENS + 4, 0:HD].astype(F32)[0:1, 0:TOK]
    scaling = 1.0 / math.sqrt(HD)
    dims = (((1,), (1,)), ((), ()))
    reached = closure(parent)
    tree_mask = jnp.concatenate([reached] * 4, axis=0) > 0.5
    tree_score = lax.dot_general(q, fresh[:, 0:HD], dims, preferred_element_type=F32) * scaling
    tree_score = jnp.where(tree_mask, tree_score, NEG)
    peak = jnp.max(tree_score, axis=1, keepdims=True)
    scores = []
    for p in range(4):
        key = got[0:32, p].reshape(256, HD)
        score = lax.dot_general(q, key, dims, preferred_element_type=F32) * scaling
        seen = iota((4 * TOK, 256), 1) < length - p * 256
        score = jnp.where(seen, score, NEG)
        peak = jnp.maximum(peak, jnp.max(score, axis=1, keepdims=True))
        scores.append(score)
    expo = jnp.where(tree_mask, jnp.exp(tree_score - peak), 0.0)
    denom = jnp.sum(expo, axis=1, keepdims=True)
    numer = jnp.dot(expo.astype(BF16), fresh[:, HD : 2 * HD], preferred_element_type=F32)
    for p in range(4):
        seen = iota((4 * TOK, 256), 1) < length - p * 256
        expo = jnp.where(seen, jnp.exp(scores[p] - peak), 0.0)
        denom = denom + jnp.sum(expo, axis=1, keepdims=True)
        value = got[32:64, p].reshape(256, HD)
        numer = numer + jnp.dot(expo.astype(BF16), value, preferred_element_type=F32)
    attention = (numer / denom).astype(BF16)
    for m in range(8):
        out[m, 0 : 4 * TOK] = attention
        out[m, 4 * TOK : 4 * TOK + 8] = fresh_rows[m]


def append_body(owner, lens, path, cache, got, out, rows):
    slots = cache.shape[0]
    depth = path.shape[0]
    for s in range(slots):
        r = jnp.maximum(owner[0, s], 0)
        count = jnp.int32(0)
        for d in range(depth):
            count = count + jnp.where(path[d, r] >= 0, 1, 0)
        count = jnp.where(owner[0, s] >= 0, count, 0)
        first = lens[r] - owner[1, s] * 256
        for y in range(8):
            rows[2 * y : 2 * y + 2] = got[y, 4 * TOK : 4 * TOK + 8].astype(F32)[2 + 2 * s : 4 + 2 * s]
        fresh = jnp.concatenate([rows[0:8], rows[8:16]], axis=1).astype(BF16)
        pick = (iota((256, depth), 0) - first == iota((256, depth), 1)).astype(BF16)
        put = jnp.dot(pick, fresh, preferred_element_type=F32).astype(BF16)
        offset = iota((256, 2 * HD), 0) - first
        out[s] = jnp.where((offset >= 0) & (offset < count), put, cache[s])


def project_body(att, first_weight, last_weight, out):
    rows = 8 * TOKENS
    own = lax.axis_index("req")
    mine = (own % 2) * 4 + own // 16
    turned = (iota((rows, 256), 0) + 4 * (mine % 2) + 6) % 8
    pick = (iota((rows, 256), 1) == turned * TOK + iota((rows, 256), 0) // 8).astype(BF16)
    parts = [att[:, g * TOK : (g + 1) * TOK].reshape(256, HD) for g in range(4)]
    both = jnp.dot(pick, jnp.concatenate(parts, axis=1), preferred_element_type=F32).astype(BF16)
    half = rows // 2
    low = iota((half, HD), 1) < 64
    dims = (((1,), (1,)), ((), ()))
    for part, weight in enumerate((first_weight, last_weight)):
        product = lax.dot_general(both, weight[...].reshape(256, 512), dims, preferred_element_type=F32)
        for i in range(4):
            x = product[:, HD * (i // 2) : HD * (i // 2) + HD]
            if i % 2 == 0:
                block = jnp.where(low, x[0:half], pltpu.roll(x[half:rows], 64, 1))
            else:
                block = jnp.where(low, pltpu.roll(x[0:half], 64, 1), x[half:rows])
            out[mine ^ ORDER[4 * part + i]] = block.astype(BF16)


def total_body(got, out):
    acc = got[0].astype(F32)
    for k in range(1, 8):
        acc = acc + got[k].astype(F32)
    acc = acc.astype(BF16)
    half = TOKENS // 2
    out[0:half] = acc[:, 0:64].reshape(half, 8, 64)
    out[half:TOKENS] = acc[:, 64:128].reshape(half, 8, 64)


VM = pl.BlockSpec(memory_space=pltpu.VMEM)
SM = pl.BlockSpec(memory_space=pltpu.SMEM)


def near(x):
    return pltpu.with_memory_space_constraint(x, pltpu.VMEM)


def call(body, name, specs, out, scratch=()):
    return pl.pallas_call(
        body,
        name=name,
        in_specs=list(specs),
        out_specs=(VM,) * len(out) if isinstance(out, tuple) else VM,
        out_shape=out,
        scratch_shapes=list(scratch),
    )


def shards(queries, tree_kv, tree_parent, accepted_path, cache_kv, piece_owner, cache_len, out_weight):
    to_all = functools.partial(lax.all_to_all, split_axis=0, concat_axis=0, tiled=True)
    spot = [[16 * (a % 4) + 2 * b + a // 4 for b in range(8)] for a in range(8)]

    def swap(x, flip):
        return lax.ppermute(x, "req", [(spot[a][b], spot[a ^ flip][b]) for a in range(8) for b in range(8)])

    owner = piece_owner.T
    path = accepted_path.T
    with jax.named_scope("weight_gather"):
        one = out_weight.T[None]
        pair = jnp.concatenate([one, swap(one, 1)])
        other_pair = swap(pair, 4)
    with jax.named_scope("spread"):
        packed, own_rows = call(
            pack_body,
            "pack",
            (SM, SM, VM, VM, VM, VM),
            (jax.ShapeDtypeStruct((64, 4, 8, HD), BF16), jax.ShapeDtypeStruct((TOK, 6 * HD), BF16)),
            [pltpu.VMEM((8, HD), F32)],
        )(owner, path, cache_kv, queries, tree_kv, tree_parent)
        pieces = to_all(packed, "req")
        pieces, pair, other_pair, own_rows = lax.optimization_barrier((pieces, pair, other_pair, own_rows))
    with jax.named_scope("route"):
        routed, fresh_rows = call(
            route_body,
            "route",
            (VM,),
            (jax.ShapeDtypeStruct((64, 4, 8, HD), BF16), pltpu.VMEM((8, 8, HD), BF16)),
            [pltpu.VMEM((4, 256), jnp.int32), pltpu.SMEM((4, 256), jnp.int32), pltpu.SemaphoreType.DMA],
        )(near(pieces))
        home = to_all(routed, "req")
        first_weight = jnp.concatenate([pair, other_pair])
        last_weight = swap(first_weight, 3)
        moves = [(r, spot[r // 8][(r + 4 * (r // 8 % 2) + 6) % 8]) for r in range(64)]
        place_rows = lax.ppermute(own_rows, "req", moves)
        home, last_weight, place_rows = lax.optimization_barrier((home, last_weight, place_rows))
    with jax.named_scope("attend"):
        attention = call(attend_body, "attend", (SM, VM, VM, VM), pltpu.VMEM((8, 4 * TOK + 8, HD), BF16))(
            cache_len, near(place_rows), near(home), near(fresh_rows)
        )
        gathered = near(to_all(attention, "req", axis_index_groups=spot))
    with jax.named_scope("append"):
        cache_out = call(
            append_body,
            "append",
            (SM, SM, SM, VM, VM),
            jax.ShapeDtypeStruct(cache_kv.shape, BF16),
            [pltpu.VMEM((16, HD), F32)],
        )(owner, cache_len, path, cache_kv, gathered)
    with jax.named_scope("project"):
        partial = call(project_body, "project", (VM, VM, VM), pltpu.VMEM((8, 4 * TOKENS, HD), BF16))(
            gathered, near(first_weight), near(last_weight)
        )
        partials = to_all(partial, "tp")
        total = call(total_body, "total", (VM,), pltpu.VMEM((TOKENS, 8, 64), BF16))(near(partials))
        pairs = [(spot[a][b] * 8 + c, spot[c][b] * 8 + a) for a in range(8) for b in range(8) for c in range(8)]
        mixed = lax.ppermute(total, ("req", "tp"), pairs)
    return (mixed.transpose(1, 0, 2), cache_out)


def solution(mesh):
    return jax.shard_map(
        shards,
        mesh=mesh,
        in_specs=(
            P("req", None, "tp"),
            P("req", None, "tp"),
            P("req", None),
            P(),
            P("req", None, "tp"),
            P("req", None),
            P(),
            P("tp", "req"),
        ),
        out_specs=(P("tp", None, "req"), P("req", None, "tp")),
        check_vma=False,
    )
```

time: 111 us -> 108 us (0.973)
  waiting for transfers between devices: 46.1 us -> 26.2 us
  blocking collectives: 21.6 us -> 37.7 us
  Pallas kernels: 10.7 us -> 9.21 us
    all_to_all x0 -> x1, blocking collectives: none -> 17.5 us  [shards(): gathered = near(to_all(attention, 'req', axis_index_groups=spot))]
    ppermute x3, waiting for transfers between devices: 17 us -> 6.16 us  [swap(): lax.ppermute(x, 'req', [(spot[a][b], spot[a ^ flip][b]) for a in range(8)...]
    all_to_all x1, waiting for transfers between devices: 8.85 us -> 0.47 us  [shards(): home = to_all(routed, 'req')]
    ppermute x1 -> x2, waiting for transfers between devices: 5.72 us -> 13.6 us  [the longest x1 8.6 us: shards(): place_rows = lax.ppermute(own_rows, 'req', moves)]
    all_to_all x1, waiting for transfers between devices: 13.6 us -> 5.93 us  [shards(): pieces = to_all(packed, 'req')]
    ppermute x1 -> x2, starting transfers between devices: 1.92 us -> 8.34 us  [the longest x1 5.43 us: shards(): place_rows = lax.ppermute(own_rows, 'req', moves)]
    all_to_all x1 -> x0, starting transfers between devices: 3.41 us -> none  [shards(): gathered = to_all(attention, 'req', axis_index_groups=spot)]
    ppermute x3, starting transfers between devices: 8.64 us -> 6.73 us  [swap(): lax.ppermute(x, 'req', [(spot[a][b], spot[a ^ flip][b]) for a in range(8)...]
  transfers between devices with their start and end apart: 7 -> 7, of which waited for: 7 -> 6; matrix products, arithmetic and copies ran while one was open for 0% -> 0% of each run, Pallas kernels for 2% -> 2%
where the time goes in v4:
time: 108 us; the launch traced here: 107 us
  blocking collectives  37.7 us (35%)
  starting transfers between devices  32.9 us (30%)
  waiting for transfers between devices  26.2 us (24%)
  Pallas kernels  9.21 us (9%)
    all_to_all x1, blocking collectives, shards(): partials = to_all(partial, 'tp')  20.2 us
    all_to_all x1, blocking collectives, shards(): gathered = near(to_all(attention, 'req', axis_index_groups=spot))  17.5 us
    all_to_all x1, starting transfers between devices, shards(): pieces = to_all(packed, 'req')  10.9 us
    ppermute x1, waiting for transfers between devices, shards(): place_rows = lax.ppermute(own_rows, 'req', moves)  8.6 us
    all_to_all x1, starting transfers between devices, shards(): home = to_all(routed, 'req')  6.9 us
    ppermute x3, starting transfers between devices, swap(): lax.ppermute(x, 'req', [(spot[a][b], spot[a ^ flip][b]) for a in range(8)...  6.73 us
    ppermute x3, waiting for transfers between devices, swap(): lax.ppermute(x, 'req', [(spot[a][b], spot[a ^ flip][b]) for a in range(8)...  6.16 us
    all_to_all x1, waiting for transfers between devices, shards(): pieces = to_all(packed, 'req')  5.93 us
  transfers between devices with their start and end apart: 7, of which 6 were waited for; matrix products, arithmetic and copies ran while one was open for 0% of the time, Pallas kernels for 2%

profile of v4, /device:TPU:6, one launch (start us, length us, event | category | flops | bytes accessed | tf_op | source)
XLA Modules:
  0.0 107.5 jit_solution(4148645917527571507)
XLA Ops:
  0.6 2.0 %pack.1 = (bf16[64,4,8,128]{3,2,1,0:T(8,128)(2,1)}, bf16[32,768]{1,0:T(8,128)(2,1)}) custom-call(s32[2,3]{1,0:T(2,128)} %bitcast.11, s32[8,64]{1,0:T(8,128)} %bitcast.9, bf16[3,256,256]{2,1,0:T(8,128)(2,1)} %cache.3, bf16[1,28,512]{2,1,0:T(8,128)(2,1)} %query.1, bf16[1,28,256]{2,1,0:T(8,128)(2,1)} %tree.1, s32[1,28]{1,0:T(1,128)} %parent.1), custom_call_target="tpu_custom_call" | custom-call | tf_op jit(solution)/shard_map/spread/pack/pallas_call | solution.py:231
  2.7 0.0 copy-start
  2.7 10.9 %all-to-all-start = ((bf16[64,4,8,128]{3,2,1,0:T(8,128)(2,1)}), bf16[64,4,8,128]{3,2,1,0:T(8,128)(2,1)S(1)}, u32[]{:S(2)}, u32[]{:S(2)}) async-start(bf16[64,4,8,128]{3,2,1,0:T(8,128)(2,1)} %get-tuple-element.13), calls=%async_computation | async-start | bytes 1048576 | tf_op jit(solution)/shard_map/spread/all_to_all | solution.py:238
  13.6 0.0 copy-done
  13.6 2.7 %collective-permute-start = (bf16[1,64,512]{2,1,0:T(8,128)(2,1)S(1)}, bf16[1,64,512]{2,1,0:T(8,128)(2,1)S(1)}, u32[]{:S(2)}, u32[]{:S(2)}) collective-permute-start(bf16[1,64,512]{2,1,0:T(8,128)(2,1)S(1)} %bitcast.6), channel_id=1, source_target_pairs={{0,128},{16,144},{32,160},{48,176},{64,192},{80,208},{96,224},{112... | collective-permute-start | bytes 196616 | tf_op jit(solution)/shard_map/weight_gather/ppermute | solution.py:222
  16.3 4.8 %collective-permute-done = bf16[1,64,512]{2,1,0:T(8,128)(2,1)S(1)} collective-permute-done((bf16[1,64,512]{2,1,0:T(8,128)(2,1)S(1)}, bf16[1,64,512]{2,1,0:T(8,128)(2,1)S(1)}, u32[]{:S(2)}, u32[]{:S(2)}) %collective-permute-start) | collective-permute-done | bytes 65568 | tf_op jit(solution)/shard_map/weight_gather/ppermute | solution.py:222
  21.1 1.9 %collective-permute-start.1 = (bf16[2,64,512]{2,1,0:T(8,128)(2,1)S(1)}, bf16[2,64,512]{2,1,0:T(8,128)(2,1)S(1)}, u32[]{:S(2)}, u32[]{:S(2)}) collective-permute-start(bf16[2,64,512]{2,1,0:T(8,128)(2,1)S(1)} %pad_maximum_fusion), channel_id=1, source_target_pairs={{0,8},{16,24},{32,40},{48,56},{64,72},{80,88},{96,104},{112,120},{... | collective-permute-start | bytes 393224 | tf_op jit(solution)/shard_map/weight_gather/ppermute | solution.py:222
  23.1 1.3 %collective-permute-done.1 = bf16[2,64,512]{2,1,0:T(8,128)(2,1)S(1)} collective-permute-done((bf16[2,64,512]{2,1,0:T(8,128)(2,1)S(1)}, bf16[2,64,512]{2,1,0:T(8,128)(2,1)S(1)}, u32[]{:S(2)}, u32[]{:S(2)}) %collective-permute-start.1) | collective-permute-done | bytes 131104 | tf_op jit(solution)/shard_map/weight_gather/ppermute | solution.py:222
  24.4 5.9 %all-to-all-done.got = bf16[64,4,8,128]{3,2,1,0:T(8,128)(2,1)S(1)} async-done(((bf16[64,4,8,128]{3,2,1,0:T(8,128)(2,1)}), bf16[64,4,8,128]{3,2,1,0:T(8,128)(2,1)S(1)}, u32[]{:S(2)}, u32[]{:S(2)}) %all-to-all-start) | async-done | bytes 524320 | tf_op jit(solution)/shard_map/spread/all_to_all | solution.py:238
  30.3 2.7 %route.1 = (bf16[64,4,8,128]{3,2,1,0:T(8,128)(2,1)}, bf16[8,8,128]{2,1,0:T(8,128)(2,1)S(1)}) custom-call(bf16[64,4,8,128]{3,2,1,0:T(8,128)(2,1)S(1)} %all-to-all-done.got), custom_call_target="tpu_custom_call" | custom-call | tf_op jit(solution)/shard_map/route/route/pallas_call | solution.py:241
  33.0 6.9 %all-to-all-start.1 = ((bf16[64,4,8,128]{3,2,1,0:T(8,128)(2,1)}), bf16[64,4,8,128]{3,2,1,0:T(8,128)(2,1)S(1)}, u32[]{:S(2)}, u32[]{:S(2)}) async-start(bf16[64,4,8,128]{3,2,1,0:T(8,128)(2,1)} %get-tuple-element.16), calls=%async_computation.1 | async-start | bytes 1048576 | tf_op jit(solution)/shard_map/route/all_to_all | solution.py:248
  40.0 0.0 copy-start.1
  40.0 2.2 %collective-permute-start.2 = (bf16[4,64,512]{2,1,0:T(8,128)(2,1)S(1)}, bf16[4,64,512]{2,1,0:T(8,128)(2,1)S(1)}, u32[]{:S(2)}, u32[]{:S(2)}) collective-permute-start(bf16[4,64,512]{2,1,0:T(8,128)(2,1)S(1)} %constant_dynamic-update-slice_fusion.first_weight), channel_id=1, source_target_pairs={{0,384},{16,400},{32,416},{48,432},{64,448},{80,464},{96,480},{112... | collective-permute-start | bytes 786440 | tf_op jit(solution)/shard_map/route/ppermute | solution.py:222
  42.1 0.0 copy-done.1
  42.2 5.4 %collective-permute-start.3 = (bf16[32,768]{1,0:T(8,128)(2,1)S(1)}, bf16[32,768]{1,0:T(8,128)(2,1)S(1)}, u32[]{:S(2)}, u32[]{:S(2)}) collective-permute-start(bf16[32,768]{1,0:T(8,128)(2,1)S(1)} %copy-done.1), channel_id=1, source_target_pairs={{0,96},{8,112},{16,0},{24,16},{32,32},{40,48},{48,64},{56,80},{64,... | collective-permute-start | bytes 147464 | tf_op jit(solution)/shard_map/route/ppermute | solution.py:252
  47.6 8.6 %collective-permute-done.3.own_rows = bf16[32,768]{1,0:T(8,128)(2,1)S(1)} collective-permute-done((bf16[32,768]{1,0:T(8,128)(2,1)S(1)}, bf16[32,768]{1,0:T(8,128)(2,1)S(1)}, u32[]{:S(2)}, u32[]{:S(2)}) %collective-permute-start.3) | collective-permute-done | bytes 49184 | tf_op jit(solution)/shard_map/route/ppermute | solution.py:252
  56.2 0.0 collective-permute-done.2.last_weight
  56.2 0.5 all-to-all-done.1.got
  56.7 1.8 %attend.1 = bf16[8,136,128]{2,1,0:T(8,128)(2,1)S(1)} custom-call(s32[64]{0:T(128)} %lens.3, bf16[32,768]{1,0:T(8,128)(2,1)S(1)} %collective-permute-done.3.own_rows, bf16[64,4,8,128]{3,2,1,0:T(8,128)(2,1)S(1)} %all-to-all-done.1.got, bf16[8,8,128]{2,1,0:T(8,128)(2,1)S(1)} %get-tuple-element.22.fresh_rows), custom_call_target="tpu_custom_call" | custom-call | tf_op jit(solution)/shard_map/attend/attend/pallas_call | solution.py:255
  58.5 17.5 %all_to_all.20.att.got = bf16[8,136,128]{2,1,0:T(8,128)(2,1)S(1)} all-to-all(bf16[8,136,128]{2,1,0:T(8,128)(2,1)S(1)} %attend.1), channel_id=1, replica_groups={{0,16,32,48,64,80,96,112},{128,144,160,176,192,208,224,240},{256,272,28..., dimensions={0} | all-to-all | bytes 557056 | tf_op jit(solution)/shard_map/attend/all_to_all | solution.py:258
  76.0 0.5 project.1
  76.5 20.2 %all_to_all.21.got = bf16[8,112,128]{2,1,0:T(8,128)(2,1)S(1)} all-to-all(bf16[8,112,128]{2,1,0:T(8,128)(2,1)S(1)} %project.1), channel_id=1, replica_groups=mesh['req'=64,'tp'=8] {'tp'}, dimensions={0} | all-to-all | bytes 458752 | tf_op jit(solution)/shard_map/project/all_to_all | solution.py:271
  96.8 0.1 total.1
  96.9 2.9 %collective-permute-start.4 = (bf16[28,8,64]{2,1,0:T(8,128)(2,1)S(1)}, bf16[28,8,64]{2,1,0:T(8,128)(2,1)S(1)}, u32[]{:S(2)}, u32[]{:S(2)}) collective-permute-start(bf16[28,8,64]{2,1,0:T(8,128)(2,1)S(1)} %total.1), channel_id=1, source_target_pairs={{0,0},{1,128},{2,256},{3,384},{4,8},{5,136},{6,264},{7,392},{16,16... | collective-permute-start | bytes 86024 | tf_op jit(solution)/shard_map/project/ppermute | solution.py:274
  99.8 2.0 %append.1 = bf16[3,256,256]{2,1,0:T(8,128)(2,1)} custom-call(s32[2,3]{1,0:T(2,128)} %bitcast.12, s32[64]{0:T(128)} %lens.3, s32[8,64]{1,0:T(8,128)} %bitcast.10, bf16[3,256,256]{2,1,0:T(8,128)(2,1)} %cache.3, bf16[8,136,128]{2,1,0:T(8,128)(2,1)S(1)} %all_to_all.20.att.got), custom_call_target="tpu_custom_call" | custom-call | tf_op jit(solution)/shard_map/append/append/pallas_call | solution.py:260
  101.8 5.0 %collective-permute-done.4 = bf16[28,8,64]{2,1,0:T(8,128)(2,1)S(1)} collective-permute-done((bf16[28,8,64]{2,1,0:T(8,128)(2,1)S(1)}, bf16[28,8,64]{2,1,0:T(8,128)(2,1)S(1)}, u32[]{:S(2)}, u32[]{:S(2)}) %collective-permute-start.4) | collective-permute-done | bytes 28704 | tf_op jit(solution)/shard_map/project/ppermute | solution.py:274
  106.8 0.6 copy.12
  (3 shorter events, 0.0 us)
Async XLA Ops:
  2.7 10.9 %copy-start = (bf16[512,64]{0,1:T(8,128)(2,1)S(1)}, bf16[512,64]{0,1:T(8,128)(2,1)}, u32[]{:S(2)}) copy-start(bf16[512,64]{0,1:T(8,128)(2,1)} %param.15) | copy-start | bytes 196612
  2.7 27.7 %all-to-all-start = ((bf16[64,4,8,128]{3,2,1,0:T(8,128)(2,1)}), bf16[64,4,8,128]{3,2,1,0:T(8,128)(2,1)S(1)}, u32[]{:S(2)}, u32[]{:S(2)}) async-start(bf16[64,4,8,128]{3,2,1,0:T(8,128)(2,1)} %get-tuple-element.13), calls=%async_computation | async-start | bytes 1048576 | tf_op jit(solution)/shard_map/spread/all_to_all | solution.py:238
  13.6 7.5 %collective-permute-start = (bf16[1,64,512]{2,1,0:T(8,128)(2,1)S(1)}, bf16[1,64,512]{2,1,0:T(8,128)(2,1)S(1)}, u32[]{:S(2)}, u32[]{:S(2)}) collective-permute-start(bf16[1,64,512]{2,1,0:T(8,128)(2,1)S(1)} %bitcast.6), channel_id=1, source_target_pairs={{0,128},{16,144},{32,160},{48,176},{64,192},{80,208},{96,224},{112... | collective-permute-start | bytes 196616 | tf_op jit(solution)/shard_map/weight_gather/ppermute | solution.py:222
  21.1 3.2 %collective-permute-start.1 = (bf16[2,64,512]{2,1,0:T(8,128)(2,1)S(1)}, bf16[2,64,512]{2,1,0:T(8,128)(2,1)S(1)}, u32[]{:S(2)}, u32[]{:S(2)}) collective-permute-start(bf16[2,64,512]{2,1,0:T(8,128)(2,1)S(1)} %pad_maximum_fusion), channel_id=1, source_target_pairs={{0,8},{16,24},{32,40},{48,56},{64,72},{80,88},{96,104},{112,120},{... | collective-permute-start | bytes 393224 | tf_op jit(solution)/shard_map/weight_gather/ppermute | solution.py:222
  33.0 23.6 %all-to-all-start.1 = ((bf16[64,4,8,128]{3,2,1,0:T(8,128)(2,1)}), bf16[64,4,8,128]{3,2,1,0:T(8,128)(2,1)S(1)}, u32[]{:S(2)}, u32[]{:S(2)}) async-start(bf16[64,4,8,128]{3,2,1,0:T(8,128)(2,1)} %get-tuple-element.16), calls=%async_computation.1 | async-start | bytes 1048576 | tf_op jit(solution)/shard_map/route/all_to_all | solution.py:248
  40.0 2.2 %copy-start.1 = (bf16[32,768]{1,0:T(8,128)(2,1)S(1)}, bf16[32,768]{1,0:T(8,128)(2,1)}, u32[]{:S(2)}) copy-start(bf16[32,768]{1,0:T(8,128)(2,1)} %get-tuple-element.19) | copy-start | bytes 147460
  40.0 16.2 %collective-permute-start.2 = (bf16[4,64,512]{2,1,0:T(8,128)(2,1)S(1)}, bf16[4,64,512]{2,1,0:T(8,128)(2,1)S(1)}, u32[]{:S(2)}, u32[]{:S(2)}) collective-permute-start(bf16[4,64,512]{2,1,0:T(8,128)(2,1)S(1)} %constant_dynamic-update-slice_fusion.first_weight), channel_id=1, source_target_pairs={{0,384},{16,400},{32,416},{48,432},{64,448},{80,464},{96,480},{112... | collective-permute-start | bytes 786440 | tf_op jit(solution)/shard_map/route/ppermute | solution.py:222
  42.2 14.0 %collective-permute-start.3 = (bf16[32,768]{1,0:T(8,128)(2,1)S(1)}, bf16[32,768]{1,0:T(8,128)(2,1)S(1)}, u32[]{:S(2)}, u32[]{:S(2)}) collective-permute-start(bf16[32,768]{1,0:T(8,128)(2,1)S(1)} %copy-done.1), channel_id=1, source_target_pairs={{0,96},{8,112},{16,0},{24,16},{32,32},{40,48},{48,64},{56,80},{64,... | collective-permute-start | bytes 147464 | tf_op jit(solution)/shard_map/route/ppermute | solution.py:252
  96.9 10.0 %collective-permute-start.4 = (bf16[28,8,64]{2,1,0:T(8,128)(2,1)S(1)}, bf16[28,8,64]{2,1,0:T(8,128)(2,1)S(1)}, u32[]{:S(2)}, u32[]{:S(2)}) collective-permute-start(bf16[28,8,64]{2,1,0:T(8,128)(2,1)S(1)} %total.1), channel_id=1, source_target_pairs={{0,0},{1,128},{2,256},{3,384},{4,8},{5,136},{6,264},{7,392},{16,16... | collective-permute-start | bytes 86024 | tf_op jit(solution)/shard_map/project/ppermute | solution.py:274

commit v5 on v4

--- a/solution.py
+++ b/solution.py
@@ -55,7 +55,7 @@
     rows[tokens : tokens + 1, 0:tokens] = parent[...].astype(F32).astype(BF16)
 
 
-def route_body(got, out, fresh, table, table_s, sem):
+def route_body(got, out, fresh, table, table_s, sem, tiles, out_sem):
     own = lax.axis_index("req")
     keys = got[:, 3, 0:1, :].astype(F32).reshape(64, HD)
     source = iota((64, 256), 0)
@@ -79,15 +79,22 @@
     def step(r, carry):
         for p in range(4):
             t = table_s[0, 4 * r + p]
-            out[r, p] = got[t >> 2, t & 3]
+            tiles[r, p] = got[t >> 2, t & 3]
         return carry
 
-    lax.fori_loop(0, 64, step, 0, unroll=8)
+    copies = []
+    for part in range(4):
+        lax.fori_loop(16 * part, 16 * part + 16, step, 0, unroll=8)
+        at = slice(16 * part, 16 * part + 16)
+        copies.append(pltpu.make_async_copy(tiles.at[at], out.at[at], out_sem.at[part]))
+        copies[-1].start()
     row = iota((8, HD), 0)
     for y in range(8):
         holder = (own // 16) * 16 + 2 * y + own % 2
-        tiles = [got[table_s[1 + i, holder], 3].astype(F32) for i in range(3)]
-        fresh[y] = jnp.where(row < 4, tiles[0], jnp.where(row < 6, tiles[1], tiles[2])).astype(BF16)
+        picks = [got[table_s[1 + i, holder], 3].astype(F32) for i in range(3)]
+        fresh[y] = jnp.where(row < 4, picks[0], jnp.where(row < 6, picks[1], picks[2])).astype(BF16)
+    for copy in copies:
+        copy.wait()
 
 
 def place_request(place):
@@ -189,26 +196,30 @@
     acc = got[0].astype(F32)
     for k in range(1, 8):
         acc = acc + got[k].astype(F32)
-    acc = acc.astype(BF16)
+    out[...] = acc.astype(BF16)
+
+
+def place_body(got, out):
     half = TOKENS // 2
-    out[0:half] = acc[:, 0:64].reshape(half, 8, 64)
-    out[half:TOKENS] = acc[:, 64:128].reshape(half, 8, 64)
+    out[0:half] = got[:, 0:64].reshape(half, 8, 64)
+    out[half:TOKENS] = got[:, 64:128].reshape(half, 8, 64)
 
 
 VM = pl.BlockSpec(memory_space=pltpu.VMEM)
 SM = pl.BlockSpec(memory_space=pltpu.SMEM)
+ANY = pl.BlockSpec(memory_space=pl.ANY)
 
 
 def near(x):
     return pltpu.with_memory_space_constraint(x, pltpu.VMEM)
 
 
-def call(body, name, specs, out, scratch=()):
+def call(body, name, specs, out, scratch=(), places=None):
     return pl.pallas_call(
         body,
         name=name,
         in_specs=list(specs),
-        out_specs=(VM,) * len(out) if isinstance(out, tuple) else VM,
+        out_specs=places or ((VM,) * len(out) if isinstance(out, tuple) else VM),
         out_shape=out,
         scratch_shapes=list(scratch),
     )
@@ -243,7 +254,14 @@
             "route",
             (VM,),
             (jax.ShapeDtypeStruct((64, 4, 8, HD), BF16), pltpu.VMEM((8, 8, HD), BF16)),
-            [pltpu.VMEM((4, 256), jnp.int32), pltpu.SMEM((4, 256), jnp.int32), pltpu.SemaphoreType.DMA],
+            [
+                pltpu.VMEM((4, 256), jnp.int32),
+                pltpu.SMEM((4, 256), jnp.int32),
+                pltpu.SemaphoreType.DMA,
+                pltpu.VMEM((64, 4, 8, HD), BF16),
+                pltpu.SemaphoreType.DMA((4,)),
+            ],
+            (ANY, VM),
         )(near(pieces))
         home = to_all(routed, "req")
         first_weight = jnp.concatenate([pair, other_pair])
@@ -269,9 +287,10 @@
             gathered, near(first_weight), near(last_weight)
         )
         partials = to_all(partial, "tp")
-        total = call(total_body, "total", (VM,), pltpu.VMEM((TOKENS, 8, 64), BF16))(near(partials))
+        total = call(total_body, "total", (VM,), pltpu.VMEM((4 * TOKENS, HD), BF16))(near(partials))
         pairs = [(spot[a][b] * 8 + c, spot[c][b] * 8 + a) for a in range(8) for b in range(8) for c in range(8)]
-        mixed = lax.ppermute(total, ("req", "tp"), pairs)
+        final = lax.ppermute(total, ("req", "tp"), pairs)
+        mixed = call(place_body, "place", (VM,), jax.ShapeDtypeStruct((TOKENS, 8, 64), BF16))(near(final))
     return (mixed.transpose(1, 0, 2), cache_out)
 
 

time: 108 us -> 108 us (level)
  no operation moved by 1% of the time
where the time goes in v5:
time: 108 us; the launch traced here: 107 us
  blocking collectives  37.7 us (35%)
  starting transfers between devices  32.9 us (30%)
  waiting for transfers between devices  25.9 us (24%)
  Pallas kernels  9.68 us (9%)
    all_to_all x1, blocking collectives, shards(): partials = to_all(partial, 'tp')  20.2 us
    all_to_all x1, blocking collectives, shards(): gathered = near(to_all(attention, 'req', axis_index_groups=spot))  17.5 us
    all_to_all x1, starting transfers between devices, shards(): pieces = to_all(packed, 'req')  10.9 us
    ppermute x1, waiting for transfers between devices, shards(): place_rows = lax.ppermute(own_rows, 'req', moves)  8.6 us
    all_to_all x1, starting transfers between devices, shards(): home = to_all(routed, 'req')  6.9 us
    ppermute x3, starting transfers between devices, swap(): lax.ppermute(x, 'req', [(spot[a][b], spot[a ^ flip][b]) for a in range(8)...  6.73 us
    ppermute x3, waiting for transfers between devices, swap(): lax.ppermute(x, 'req', [(spot[a][b], spot[a ^ flip][b]) for a in range(8)...  6.16 us
    all_to_all x1, waiting for transfers between devices, shards(): pieces = to_all(packed, 'req')  5.93 us
  transfers between devices with their start and end apart: 7, of which 6 were waited for; matrix products, arithmetic and copies ran while one was open for 0% of the time, Pallas kernels for 2%

profile of v5, /device:TPU:6, one launch (start us, length us, event | category | flops | bytes accessed | tf_op | source)
XLA Modules:
  0.0 107.0 jit_solution(7935539595452470295)
XLA Ops:
  0.6 2.0 %pack.1 = (bf16[64,4,8,128]{3,2,1,0:T(8,128)(2,1)}, bf16[32,768]{1,0:T(8,128)(2,1)}) custom-call(s32[2,3]{1,0:T(2,128)} %bitcast.11, s32[8,64]{1,0:T(8,128)} %bitcast.9, bf16[3,256,256]{2,1,0:T(8,128)(2,1)} %cache.3, bf16[1,28,512]{2,1,0:T(8,128)(2,1)} %query.1, bf16[1,28,256]{2,1,0:T(8,128)(2,1)} %tree.1, s32[1,28]{1,0:T(1,128)} %parent.1), custom_call_target="tpu_custom_call" | custom-call | tf_op jit(solution)/shard_map/spread/pack/pallas_call | solution.py:242
  2.7 0.0 copy-start
  2.7 10.9 %all-to-all-start = ((bf16[64,4,8,128]{3,2,1,0:T(8,128)(2,1)}), bf16[64,4,8,128]{3,2,1,0:T(8,128)(2,1)S(1)}, u32[]{:S(2)}, u32[]{:S(2)}) async-start(bf16[64,4,8,128]{3,2,1,0:T(8,128)(2,1)} %get-tuple-element.13), calls=%async_computation | async-start | bytes 1048576 | tf_op jit(solution)/shard_map/spread/all_to_all | solution.py:249
  13.6 0.0 copy-done
  13.6 2.7 %collective-permute-start = (bf16[1,64,512]{2,1,0:T(8,128)(2,1)S(1)}, bf16[1,64,512]{2,1,0:T(8,128)(2,1)S(1)}, u32[]{:S(2)}, u32[]{:S(2)}) collective-permute-start(bf16[1,64,512]{2,1,0:T(8,128)(2,1)S(1)} %bitcast.6), channel_id=1, source_target_pairs={{0,128},{16,144},{32,160},{48,176},{64,192},{80,208},{96,224},{112... | collective-permute-start | bytes 196616 | tf_op jit(solution)/shard_map/weight_gather/ppermute | solution.py:233
  16.3 4.8 %collective-permute-done = bf16[1,64,512]{2,1,0:T(8,128)(2,1)S(1)} collective-permute-done((bf16[1,64,512]{2,1,0:T(8,128)(2,1)S(1)}, bf16[1,64,512]{2,1,0:T(8,128)(2,1)S(1)}, u32[]{:S(2)}, u32[]{:S(2)}) %collective-permute-start) | collective-permute-done | bytes 65568 | tf_op jit(solution)/shard_map/weight_gather/ppermute | solution.py:233
  21.1 1.9 %collective-permute-start.1 = (bf16[2,64,512]{2,1,0:T(8,128)(2,1)S(1)}, bf16[2,64,512]{2,1,0:T(8,128)(2,1)S(1)}, u32[]{:S(2)}, u32[]{:S(2)}) collective-permute-start(bf16[2,64,512]{2,1,0:T(8,128)(2,1)S(1)} %pad_maximum_fusion), channel_id=1, source_target_pairs={{0,8},{16,24},{32,40},{48,56},{64,72},{80,88},{96,104},{112,120},{... | collective-permute-start | bytes 393224 | tf_op jit(solution)/shard_map/weight_gather/ppermute | solution.py:233
  23.1 1.3 %collective-permute-done.1 = bf16[2,64,512]{2,1,0:T(8,128)(2,1)S(1)} collective-permute-done((bf16[2,64,512]{2,1,0:T(8,128)(2,1)S(1)}, bf16[2,64,512]{2,1,0:T(8,128)(2,1)S(1)}, u32[]{:S(2)}, u32[]{:S(2)}) %collective-permute-start.1) | collective-permute-done | bytes 131104 | tf_op jit(solution)/shard_map/weight_gather/ppermute | solution.py:233
  24.4 5.9 %all-to-all-done.got = bf16[64,4,8,128]{3,2,1,0:T(8,128)(2,1)S(1)} async-done(((bf16[64,4,8,128]{3,2,1,0:T(8,128)(2,1)}), bf16[64,4,8,128]{3,2,1,0:T(8,128)(2,1)S(1)}, u32[]{:S(2)}, u32[]{:S(2)}) %all-to-all-start) | async-done | bytes 524320 | tf_op jit(solution)/shard_map/spread/all_to_all | solution.py:249
  30.3 2.5 %route.1 = (bf16[64,4,8,128]{3,2,1,0:T(8,128)(2,1)}, bf16[8,8,128]{2,1,0:T(8,128)(2,1)S(1)}) custom-call(bf16[64,4,8,128]{3,2,1,0:T(8,128)(2,1)S(1)} %all-to-all-done.got), custom_call_target="tpu_custom_call" | custom-call | tf_op jit(solution)/shard_map/route/route/pallas_call | solution.py:252
  32.9 6.9 %all-to-all-start.1 = ((bf16[64,4,8,128]{3,2,1,0:T(8,128)(2,1)}), bf16[64,4,8,128]{3,2,1,0:T(8,128)(2,1)S(1)}, u32[]{:S(2)}, u32[]{:S(2)}) async-start(bf16[64,4,8,128]{3,2,1,0:T(8,128)(2,1)} %get-tuple-element.16), calls=%async_computation.1 | async-start | bytes 1048576 | tf_op jit(solution)/shard_map/route/all_to_all | solution.py:266
  39.8 0.0 copy-start.1
  39.8 2.2 %collective-permute-start.2 = (bf16[4,64,512]{2,1,0:T(8,128)(2,1)S(1)}, bf16[4,64,512]{2,1,0:T(8,128)(2,1)S(1)}, u32[]{:S(2)}, u32[]{:S(2)}) collective-permute-start(bf16[4,64,512]{2,1,0:T(8,128)(2,1)S(1)} %constant_dynamic-update-slice_fusion.first_weight), channel_id=1, source_target_pairs={{0,384},{16,400},{32,416},{48,432},{64,448},{80,464},{96,480},{112... | collective-permute-start | bytes 786440 | tf_op jit(solution)/shard_map/route/ppermute | solution.py:233
  42.0 0.0 copy-done.1
  42.0 5.4 %collective-permute-start.3 = (bf16[32,768]{1,0:T(8,128)(2,1)S(1)}, bf16[32,768]{1,0:T(8,128)(2,1)S(1)}, u32[]{:S(2)}, u32[]{:S(2)}) collective-permute-start(bf16[32,768]{1,0:T(8,128)(2,1)S(1)} %copy-done.1), channel_id=1, source_target_pairs={{0,96},{8,112},{16,0},{24,16},{32,32},{40,48},{48,64},{56,80},{64,... | collective-permute-start | bytes 147464 | tf_op jit(solution)/shard_map/route/ppermute | solution.py:270
  47.4 8.6 %collective-permute-done.3.own_rows = bf16[32,768]{1,0:T(8,128)(2,1)S(1)} collective-permute-done((bf16[32,768]{1,0:T(8,128)(2,1)S(1)}, bf16[32,768]{1,0:T(8,128)(2,1)S(1)}, u32[]{:S(2)}, u32[]{:S(2)}) %collective-permute-start.3) | collective-permute-done | bytes 49184 | tf_op jit(solution)/shard_map/route/ppermute | solution.py:270
  56.0 0.0 collective-permute-done.2.last_weight
  56.0 0.5 all-to-all-done.1.got
  56.5 1.8 %attend.1 = bf16[8,136,128]{2,1,0:T(8,128)(2,1)S(1)} custom-call(s32[64]{0:T(128)} %lens.3, bf16[32,768]{1,0:T(8,128)(2,1)S(1)} %collective-permute-done.3.own_rows, bf16[64,4,8,128]{3,2,1,0:T(8,128)(2,1)S(1)} %all-to-all-done.1.got, bf16[8,8,128]{2,1,0:T(8,128)(2,1)S(1)} %get-tuple-element.22.fresh_rows), custom_call_target="tpu_custom_call" | custom-call | tf_op jit(solution)/shard_map/attend/attend/pallas_call | solution.py:273
  58.3 17.5 %all_to_all.20.att.got = bf16[8,136,128]{2,1,0:T(8,128)(2,1)S(1)} all-to-all(bf16[8,136,128]{2,1,0:T(8,128)(2,1)S(1)} %attend.1), channel_id=1, replica_groups={{0,16,32,48,64,80,96,112},{128,144,160,176,192,208,224,240},{256,272,28..., dimensions={0} | all-to-all | bytes 557056 | tf_op jit(solution)/shard_map/attend/all_to_all | solution.py:276
  75.8 0.5 project.1
  76.4 20.2 %all_to_all.21.got = bf16[8,112,128]{2,1,0:T(8,128)(2,1)S(1)} all-to-all(bf16[8,112,128]{2,1,0:T(8,128)(2,1)S(1)} %project.1), channel_id=1, replica_groups=mesh['req'=64,'tp'=8] {'tp'}, dimensions={0} | all-to-all | bytes 458752 | tf_op jit(solution)/shard_map/project/all_to_all | solution.py:289
  96.6 2.9 %collective-permute-start.4 = (bf16[112,128]{1,0:T(8,128)(2,1)S(1)}, bf16[112,128]{1,0:T(8,128)(2,1)S(1)}, u32[]{:S(2)}, u32[]{:S(2)}) collective-permute-start(bf16[112,128]{1,0:T(8,128)(2,1)S(1)} %total.1), channel_id=1, source_target_pairs={{0,0},{1,128},{2,256},{3,384},{4,8},{5,136},{6,264},{7,392},{16,16... | collective-permute-start | bytes 86024 | tf_op jit(solution)/shard_map/project/ppermute | solution.py:292
  99.6 2.0 %append.1 = bf16[3,256,256]{2,1,0:T(8,128)(2,1)} custom-call(s32[2,3]{1,0:T(2,128)} %bitcast.12, s32[64]{0:T(128)} %lens.3, s32[8,64]{1,0:T(8,128)} %bitcast.10, bf16[3,256,256]{2,1,0:T(8,128)(2,1)} %cache.3, bf16[8,136,128]{2,1,0:T(8,128)(2,1)S(1)} %all_to_all.20.att.got), custom_call_target="tpu_custom_call" | custom-call | tf_op jit(solution)/shard_map/append/append/pallas_call | solution.py:278
  101.6 4.7 %collective-permute-done.4.got = bf16[112,128]{1,0:T(8,128)(2,1)S(1)} collective-permute-done((bf16[112,128]{1,0:T(8,128)(2,1)S(1)}, bf16[112,128]{1,0:T(8,128)(2,1)S(1)}, u32[]{:S(2)}, u32[]{:S(2)}) %collective-permute-start.4) | collective-permute-done | bytes 28704 | tf_op jit(solution)/shard_map/project/ppermute | solution.py:292
  106.3 0.7 place.1
  (4 shorter events, 0.1 us)
Async XLA Ops:
  2.7 10.9 %copy-start = (bf16[512,64]{0,1:T(8,128)(2,1)S(1)}, bf16[512,64]{0,1:T(8,128)(2,1)}, u32[]{:S(2)}) copy-start(bf16[512,64]{0,1:T(8,128)(2,1)} %param.15) | copy-start | bytes 196612
  2.7 27.7 %all-to-all-start = ((bf16[64,4,8,128]{3,2,1,0:T(8,128)(2,1)}), bf16[64,4,8,128]{3,2,1,0:T(8,128)(2,1)S(1)}, u32[]{:S(2)}, u32[]{:S(2)}) async-start(bf16[64,4,8,128]{3,2,1,0:T(8,128)(2,1)} %get-tuple-element.13), calls=%async_computation | async-start | bytes 1048576 | tf_op jit(solution)/shard_map/spread/all_to_all | solution.py:249
  13.6 7.5 %collective-permute-start = (bf16[1,64,512]{2,1,0:T(8,128)(2,1)S(1)}, bf16[1,64,512]{2,1,0:T(8,128)(2,1)S(1)}, u32[]{:S(2)}, u32[]{:S(2)}) collective-permute-start(bf16[1,64,512]{2,1,0:T(8,128)(2,1)S(1)} %bitcast.6), channel_id=1, source_target_pairs={{0,128},{16,144},{32,160},{48,176},{64,192},{80,208},{96,224},{112... | collective-permute-start | bytes 196616 | tf_op jit(solution)/shard_map/weight_gather/ppermute | solution.py:233
  21.1 3.2 %collective-permute-start.1 = (bf16[2,64,512]{2,1,0:T(8,128)(2,1)S(1)}, bf16[2,64,512]{2,1,0:T(8,128)(2,1)S(1)}, u32[]{:S(2)}, u32[]{:S(2)}) collective-permute-start(bf16[2,64,512]{2,1,0:T(8,128)(2,1)S(1)} %pad_maximum_fusion), channel_id=1, source_target_pairs={{0,8},{16,24},{32,40},{48,56},{64,72},{80,88},{96,104},{112,120},{... | collective-permute-start | bytes 393224 | tf_op jit(solution)/shard_map/weight_gather/ppermute | solution.py:233
  32.9 23.6 %all-to-all-start.1 = ((bf16[64,4,8,128]{3,2,1,0:T(8,128)(2,1)}), bf16[64,4,8,128]{3,2,1,0:T(8,128)(2,1)S(1)}, u32[]{:S(2)}, u32[]{:S(2)}) async-start(bf16[64,4,8,128]{3,2,1,0:T(8,128)(2,1)} %get-tuple-element.16), calls=%async_computation.1 | async-start | bytes 1048576 | tf_op jit(solution)/shard_map/route/all_to_all | solution.py:266
  39.8 2.2 %copy-start.1 = (bf16[32,768]{1,0:T(8,128)(2,1)S(1)}, bf16[32,768]{1,0:T(8,128)(2,1)}, u32[]{:S(2)}) copy-start(bf16[32,768]{1,0:T(8,128)(2,1)} %get-tuple-element.19) | copy-start | bytes 147460
  39.8 16.2 %collective-permute-start.2 = (bf16[4,64,512]{2,1,0:T(8,128)(2,1)S(1)}, bf16[4,64,512]{2,1,0:T(8,128)(2,1)S(1)}, u32[]{:S(2)}, u32[]{:S(2)}) collective-permute-start(bf16[4,64,512]{2,1,0:T(8,128)(2,1)S(1)} %constant_dynamic-update-slice_fusion.first_weight), channel_id=1, source_target_pairs={{0,384},{16,400},{32,416},{48,432},{64,448},{80,464},{96,480},{112... | collective-permute-start | bytes 786440 | tf_op jit(solution)/shard_map/route/ppermute | solution.py:233
  42.0 14.0 %collective-permute-start.3 = (bf16[32,768]{1,0:T(8,128)(2,1)S(1)}, bf16[32,768]{1,0:T(8,128)(2,1)S(1)}, u32[]{:S(2)}, u32[]{:S(2)}) collective-permute-start(bf16[32,768]{1,0:T(8,128)(2,1)S(1)} %copy-done.1), channel_id=1, source_target_pairs={{0,96},{8,112},{16,0},{24,16},{32,32},{40,48},{48,64},{56,80},{64,... | collective-permute-start | bytes 147464 | tf_op jit(solution)/shard_map/route/ppermute | solution.py:270
  96.6 9.7 %collective-permute-start.4 = (bf16[112,128]{1,0:T(8,128)(2,1)S(1)}, bf16[112,128]{1,0:T(8,128)(2,1)S(1)}, u32[]{:S(2)}, u32[]{:S(2)}) collective-permute-start(bf16[112,128]{1,0:T(8,128)(2,1)S(1)} %total.1), channel_id=1, source_target_pairs={{0,0},{1,128},{2,256},{3,384},{4,8},{5,136},{6,264},{7,392},{16,16... | collective-permute-start | bytes 86024 | tf_op jit(solution)/shard_map/project/ppermute | solution.py:292

commit v6 on v5

--- a/solution.py
+++ b/solution.py
@@ -84,7 +84,7 @@
 
     copies = []
     for part in range(4):
-        lax.fori_loop(16 * part, 16 * part + 16, step, 0, unroll=8)
+        lax.fori_loop(16 * part, 16 * part + 16, step, 0, unroll=16)
         at = slice(16 * part, 16 * part + 16)
         copies.append(pltpu.make_async_copy(tiles.at[at], out.at[at], out_sem.at[part]))
         copies[-1].start()
@@ -139,12 +139,13 @@
     expo = jnp.where(tree_mask, jnp.exp(tree_score - peak), 0.0)
     denom = jnp.sum(expo, axis=1, keepdims=True)
     numer = jnp.dot(expo.astype(BF16), fresh[:, HD : 2 * HD], preferred_element_type=F32)
+    total = jnp.zeros((4 * TOK, 256), F32)
     for p in range(4):
-        seen = iota((4 * TOK, 256), 1) < length - p * 256
-        expo = jnp.where(seen, jnp.exp(scores[p] - peak), 0.0)
-        denom = denom + jnp.sum(expo, axis=1, keepdims=True)
+        expo = jnp.exp(scores[p] - peak)
+        total = total + expo
         value = got[32:64, p].reshape(256, HD)
         numer = numer + jnp.dot(expo.astype(BF16), value, preferred_element_type=F32)
+    denom = denom + jnp.sum(total, axis=1, keepdims=True)
     attention = (numer / denom).astype(BF16)
     for m in range(8):
         out[m, 0 : 4 * TOK] = attention

time: 108 us -> 107 us (level)
  no operation moved by 1% of the time
where the time goes in v6:
time: 107 us
  blocking collectives  37.7 us (35%)
  starting transfers between devices  32.9 us (31%)
  waiting for transfers between devices  25.9 us (24%)
  Pallas kernels  9.33 us (9%)
    all_to_all x1, blocking collectives, shards(): partials = to_all(partial, 'tp')  20.3 us
    all_to_all x1, blocking collectives, shards(): gathered = near(to_all(attention, 'req', axis_index_groups=spot))  17.5 us
    all_to_all x1, starting transfers between devices, shards(): pieces = to_all(packed, 'req')  10.9 us
    ppermute x1, waiting for transfers between devices, shards(): place_rows = lax.ppermute(own_rows, 'req', moves)  8.6 us
    all_to_all x1, starting transfers between devices, shards(): home = to_all(routed, 'req')  6.9 us
    ppermute x3, starting transfers between devices, swap(): lax.ppermute(x, 'req', [(spot[a][b], spot[a ^ flip][b]) for a in range(8)...  6.73 us
    ppermute x3, waiting for transfers between devices, swap(): lax.ppermute(x, 'req', [(spot[a][b], spot[a ^ flip][b]) for a in range(8)...  6.16 us
    all_to_all x1, waiting for transfers between devices, shards(): pieces = to_all(packed, 'req')  5.93 us
  transfers between devices with their start and end apart: 7, of which 6 were waited for; matrix products, arithmetic and copies ran while one was open for 0% of the time, Pallas kernels for 2%

profile of v6, /device:TPU:6, one launch (start us, length us, event | category | flops | bytes accessed | tf_op | source)
XLA Modules:
  0.0 106.7 jit_solution(9271367972588346255)
XLA Ops:
  0.6 2.0 %pack.1 = (bf16[64,4,8,128]{3,2,1,0:T(8,128)(2,1)}, bf16[32,768]{1,0:T(8,128)(2,1)}) custom-call(s32[2,3]{1,0:T(2,128)} %bitcast.11, s32[8,64]{1,0:T(8,128)} %bitcast.9, bf16[3,256,256]{2,1,0:T(8,128)(2,1)} %cache.3, bf16[1,28,512]{2,1,0:T(8,128)(2,1)} %query.1, bf16[1,28,256]{2,1,0:T(8,128)(2,1)} %tree.1, s32[1,28]{1,0:T(1,128)} %parent.1), custom_call_target="tpu_custom_call" | custom-call | tf_op jit(solution)/shard_map/spread/pack/pallas_call | solution.py:243
  2.7 0.0 copy-start
  2.7 10.9 %all-to-all-start = ((bf16[64,4,8,128]{3,2,1,0:T(8,128)(2,1)}), bf16[64,4,8,128]{3,2,1,0:T(8,128)(2,1)S(1)}, u32[]{:S(2)}, u32[]{:S(2)}) async-start(bf16[64,4,8,128]{3,2,1,0:T(8,128)(2,1)} %get-tuple-element.13), calls=%async_computation | async-start | bytes 1048576 | tf_op jit(solution)/shard_map/spread/all_to_all | solution.py:250
  13.6 0.0 copy-done
  13.6 2.7 %collective-permute-start = (bf16[1,64,512]{2,1,0:T(8,128)(2,1)S(1)}, bf16[1,64,512]{2,1,0:T(8,128)(2,1)S(1)}, u32[]{:S(2)}, u32[]{:S(2)}) collective-permute-start(bf16[1,64,512]{2,1,0:T(8,128)(2,1)S(1)} %bitcast.6), channel_id=1, source_target_pairs={{0,128},{16,144},{32,160},{48,176},{64,192},{80,208},{96,224},{112... | collective-permute-start | bytes 196616 | tf_op jit(solution)/shard_map/weight_gather/ppermute | solution.py:234
  16.3 4.8 %collective-permute-done = bf16[1,64,512]{2,1,0:T(8,128)(2,1)S(1)} collective-permute-done((bf16[1,64,512]{2,1,0:T(8,128)(2,1)S(1)}, bf16[1,64,512]{2,1,0:T(8,128)(2,1)S(1)}, u32[]{:S(2)}, u32[]{:S(2)}) %collective-permute-start) | collective-permute-done | bytes 65568 | tf_op jit(solution)/shard_map/weight_gather/ppermute | solution.py:234
  21.1 1.9 %collective-permute-start.1 = (bf16[2,64,512]{2,1,0:T(8,128)(2,1)S(1)}, bf16[2,64,512]{2,1,0:T(8,128)(2,1)S(1)}, u32[]{:S(2)}, u32[]{:S(2)}) collective-permute-start(bf16[2,64,512]{2,1,0:T(8,128)(2,1)S(1)} %pad_maximum_fusion), channel_id=1, source_target_pairs={{0,8},{16,24},{32,40},{48,56},{64,72},{80,88},{96,104},{112,120},{... | collective-permute-start | bytes 393224 | tf_op jit(solution)/shard_map/weight_gather/ppermute | solution.py:234
  23.1 1.3 %collective-permute-done.1 = bf16[2,64,512]{2,1,0:T(8,128)(2,1)S(1)} collective-permute-done((bf16[2,64,512]{2,1,0:T(8,128)(2,1)S(1)}, bf16[2,64,512]{2,1,0:T(8,128)(2,1)S(1)}, u32[]{:S(2)}, u32[]{:S(2)}) %collective-permute-start.1) | collective-permute-done | bytes 131104 | tf_op jit(solution)/shard_map/weight_gather/ppermute | solution.py:234
  24.4 5.9 %all-to-all-done.got = bf16[64,4,8,128]{3,2,1,0:T(8,128)(2,1)S(1)} async-done(((bf16[64,4,8,128]{3,2,1,0:T(8,128)(2,1)}), bf16[64,4,8,128]{3,2,1,0:T(8,128)(2,1)S(1)}, u32[]{:S(2)}, u32[]{:S(2)}) %all-to-all-start) | async-done | bytes 524320 | tf_op jit(solution)/shard_map/spread/all_to_all | solution.py:250
  30.3 2.2 %route.1 = (bf16[64,4,8,128]{3,2,1,0:T(8,128)(2,1)}, bf16[8,8,128]{2,1,0:T(8,128)(2,1)S(1)}) custom-call(bf16[64,4,8,128]{3,2,1,0:T(8,128)(2,1)S(1)} %all-to-all-done.got), custom_call_target="tpu_custom_call" | custom-call | tf_op jit(solution)/shard_map/route/route/pallas_call | solution.py:253
  32.5 6.9 %all-to-all-start.1 = ((bf16[64,4,8,128]{3,2,1,0:T(8,128)(2,1)}), bf16[64,4,8,128]{3,2,1,0:T(8,128)(2,1)S(1)}, u32[]{:S(2)}, u32[]{:S(2)}) async-start(bf16[64,4,8,128]{3,2,1,0:T(8,128)(2,1)} %get-tuple-element.16), calls=%async_computation.1 | async-start | bytes 1048576 | tf_op jit(solution)/shard_map/route/all_to_all | solution.py:267
  39.4 0.0 copy-start.1
  39.5 2.2 %collective-permute-start.2 = (bf16[4,64,512]{2,1,0:T(8,128)(2,1)S(1)}, bf16[4,64,512]{2,1,0:T(8,128)(2,1)S(1)}, u32[]{:S(2)}, u32[]{:S(2)}) collective-permute-start(bf16[4,64,512]{2,1,0:T(8,128)(2,1)S(1)} %constant_dynamic-update-slice_fusion.first_weight), channel_id=1, source_target_pairs={{0,384},{16,400},{32,416},{48,432},{64,448},{80,464},{96,480},{112... | collective-permute-start | bytes 786440 | tf_op jit(solution)/shard_map/route/ppermute | solution.py:234
  41.6 0.0 copy-done.1
  41.6 5.4 %collective-permute-start.3 = (bf16[32,768]{1,0:T(8,128)(2,1)S(1)}, bf16[32,768]{1,0:T(8,128)(2,1)S(1)}, u32[]{:S(2)}, u32[]{:S(2)}) collective-permute-start(bf16[32,768]{1,0:T(8,128)(2,1)S(1)} %copy-done.1), channel_id=1, source_target_pairs={{0,96},{8,112},{16,0},{24,16},{32,32},{40,48},{48,64},{56,80},{64,... | collective-permute-start | bytes 147464 | tf_op jit(solution)/shard_map/route/ppermute | solution.py:271
  47.1 8.6 %collective-permute-done.3.own_rows = bf16[32,768]{1,0:T(8,128)(2,1)S(1)} collective-permute-done((bf16[32,768]{1,0:T(8,128)(2,1)S(1)}, bf16[32,768]{1,0:T(8,128)(2,1)S(1)}, u32[]{:S(2)}, u32[]{:S(2)}) %collective-permute-start.3) | collective-permute-done | bytes 49184 | tf_op jit(solution)/shard_map/route/ppermute | solution.py:271
  55.7 0.0 collective-permute-done.2.last_weight
  55.7 0.5 all-to-all-done.1.got
  56.1 1.9 %attend.1 = bf16[8,136,128]{2,1,0:T(8,128)(2,1)S(1)} custom-call(s32[64]{0:T(128)} %lens.3, bf16[32,768]{1,0:T(8,128)(2,1)S(1)} %collective-permute-done.3.own_rows, bf16[64,4,8,128]{3,2,1,0:T(8,128)(2,1)S(1)} %all-to-all-done.1.got, bf16[8,8,128]{2,1,0:T(8,128)(2,1)S(1)} %get-tuple-element.22.fresh_rows), custom_call_target="tpu_custom_call" | custom-call | tf_op jit(solution)/shard_map/attend/attend/pallas_call | solution.py:274
  58.0 17.5 %all_to_all.20.att.got = bf16[8,136,128]{2,1,0:T(8,128)(2,1)S(1)} all-to-all(bf16[8,136,128]{2,1,0:T(8,128)(2,1)S(1)} %attend.1), channel_id=1, replica_groups={{0,16,32,48,64,80,96,112},{128,144,160,176,192,208,224,240},{256,272,28..., dimensions={0} | all-to-all | bytes 557056 | tf_op jit(solution)/shard_map/attend/all_to_all | solution.py:277
  75.5 0.5 project.1
  76.0 20.3 %all_to_all.21.got = bf16[8,112,128]{2,1,0:T(8,128)(2,1)S(1)} all-to-all(bf16[8,112,128]{2,1,0:T(8,128)(2,1)S(1)} %project.1), channel_id=1, replica_groups=mesh['req'=64,'tp'=8] {'tp'}, dimensions={0} | all-to-all | bytes 458752 | tf_op jit(solution)/shard_map/project/all_to_all | solution.py:290
  96.3 2.9 %collective-permute-start.4 = (bf16[112,128]{1,0:T(8,128)(2,1)S(1)}, bf16[112,128]{1,0:T(8,128)(2,1)S(1)}, u32[]{:S(2)}, u32[]{:S(2)}) collective-permute-start(bf16[112,128]{1,0:T(8,128)(2,1)S(1)} %total.1), channel_id=1, source_target_pairs={{0,0},{1,128},{2,256},{3,384},{4,8},{5,136},{6,264},{7,392},{16,16... | collective-permute-start | bytes 86024 | tf_op jit(solution)/shard_map/project/ppermute | solution.py:293
  99.2 2.0 %append.1 = bf16[3,256,256]{2,1,0:T(8,128)(2,1)} custom-call(s32[2,3]{1,0:T(2,128)} %bitcast.12, s32[64]{0:T(128)} %lens.3, s32[8,64]{1,0:T(8,128)} %bitcast.10, bf16[3,256,256]{2,1,0:T(8,128)(2,1)} %cache.3, bf16[8,136,128]{2,1,0:T(8,128)(2,1)S(1)} %all_to_all.20.att.got), custom_call_target="tpu_custom_call" | custom-call | tf_op jit(solution)/shard_map/append/append/pallas_call | solution.py:279
  101.3 4.7 %collective-permute-done.4.got = bf16[112,128]{1,0:T(8,128)(2,1)S(1)} collective-permute-done((bf16[112,128]{1,0:T(8,128)(2,1)S(1)}, bf16[112,128]{1,0:T(8,128)(2,1)S(1)}, u32[]{:S(2)}, u32[]{:S(2)}) %collective-permute-start.4) | collective-permute-done | bytes 28704 | tf_op jit(solution)/shard_map/project/ppermute | solution.py:293
  106.0 0.7 place.1
  (4 shorter events, 0.1 us)
Async XLA Ops:
  2.7 10.9 %copy-start = (bf16[512,64]{0,1:T(8,128)(2,1)S(1)}, bf16[512,64]{0,1:T(8,128)(2,1)}, u32[]{:S(2)}) copy-start(bf16[512,64]{0,1:T(8,128)(2,1)} %param.15) | copy-start | bytes 196612
  2.7 27.7 %all-to-all-start = ((bf16[64,4,8,128]{3,2,1,0:T(8,128)(2,1)}), bf16[64,4,8,128]{3,2,1,0:T(8,128)(2,1)S(1)}, u32[]{:S(2)}, u32[]{:S(2)}) async-start(bf16[64,4,8,128]{3,2,1,0:T(8,128)(2,1)} %get-tuple-element.13), calls=%async_computation | async-start | bytes 1048576 | tf_op jit(solution)/shard_map/spread/all_to_all | solution.py:250
  13.6 7.5 %collective-permute-start = (bf16[1,64,512]{2,1,0:T(8,128)(2,1)S(1)}, bf16[1,64,512]{2,1,0:T(8,128)(2,1)S(1)}, u32[]{:S(2)}, u32[]{:S(2)}) collective-permute-start(bf16[1,64,512]{2,1,0:T(8,128)(2,1)S(1)} %bitcast.6), channel_id=1, source_target_pairs={{0,128},{16,144},{32,160},{48,176},{64,192},{80,208},{96,224},{112... | collective-permute-start | bytes 196616 | tf_op jit(solution)/shard_map/weight_gather/ppermute | solution.py:234
  21.1 3.2 %collective-permute-start.1 = (bf16[2,64,512]{2,1,0:T(8,128)(2,1)S(1)}, bf16[2,64,512]{2,1,0:T(8,128)(2,1)S(1)}, u32[]{:S(2)}, u32[]{:S(2)}) collective-permute-start(bf16[2,64,512]{2,1,0:T(8,128)(2,1)S(1)} %pad_maximum_fusion), channel_id=1, source_target_pairs={{0,8},{16,24},{32,40},{48,56},{64,72},{80,88},{96,104},{112,120},{... | collective-permute-start | bytes 393224 | tf_op jit(solution)/shard_map/weight_gather/ppermute | solution.py:234
  32.5 23.6 %all-to-all-start.1 = ((bf16[64,4,8,128]{3,2,1,0:T(8,128)(2,1)}), bf16[64,4,8,128]{3,2,1,0:T(8,128)(2,1)S(1)}, u32[]{:S(2)}, u32[]{:S(2)}) async-start(bf16[64,4,8,128]{3,2,1,0:T(8,128)(2,1)} %get-tuple-element.16), calls=%async_computation.1 | async-start | bytes 1048576 | tf_op jit(solution)/shard_map/route/all_to_all | solution.py:267
  39.4 2.2 %copy-start.1 = (bf16[32,768]{1,0:T(8,128)(2,1)S(1)}, bf16[32,768]{1,0:T(8,128)(2,1)}, u32[]{:S(2)}) copy-start(bf16[32,768]{1,0:T(8,128)(2,1)} %get-tuple-element.19) | copy-start | bytes 147460
  39.5 16.2 %collective-permute-start.2 = (bf16[4,64,512]{2,1,0:T(8,128)(2,1)S(1)}, bf16[4,64,512]{2,1,0:T(8,128)(2,1)S(1)}, u32[]{:S(2)}, u32[]{:S(2)}) collective-permute-start(bf16[4,64,512]{2,1,0:T(8,128)(2,1)S(1)} %constant_dynamic-update-slice_fusion.first_weight), channel_id=1, source_target_pairs={{0,384},{16,400},{32,416},{48,432},{64,448},{80,464},{96,480},{112... | collective-permute-start | bytes 786440 | tf_op jit(solution)/shard_map/route/ppermute | solution.py:234
  41.6 14.0 %collective-permute-start.3 = (bf16[32,768]{1,0:T(8,128)(2,1)S(1)}, bf16[32,768]{1,0:T(8,128)(2,1)S(1)}, u32[]{:S(2)}, u32[]{:S(2)}) collective-permute-start(bf16[32,768]{1,0:T(8,128)(2,1)S(1)} %copy-done.1), channel_id=1, source_target_pairs={{0,96},{8,112},{16,0},{24,16},{32,32},{40,48},{48,64},{56,80},{64,... | collective-permute-start | bytes 147464 | tf_op jit(solution)/shard_map/route/ppermute | solution.py:271
  96.3 9.7 %collective-permute-start.4 = (bf16[112,128]{1,0:T(8,128)(2,1)S(1)}, bf16[112,128]{1,0:T(8,128)(2,1)S(1)}, u32[]{:S(2)}, u32[]{:S(2)}) collective-permute-start(bf16[112,128]{1,0:T(8,128)(2,1)S(1)} %total.1), channel_id=1, source_target_pairs={{0,0},{1,128},{2,256},{3,384},{4,8},{5,136},{6,264},{7,392},{16,16... | collective-permute-start | bytes 86024 | tf_op jit(solution)/shard_map/project/ppermute | solution.py:293

commit v7 on v6

--- a/solution.py
+++ b/solution.py
@@ -62,14 +62,16 @@
     lane = iota((64, 256), 1)
     target = (place_request(lane // 4) * 4 + lane % 4).astype(F32)
     tile = (source * 4).astype(F32)
-    diagonal = source == lane
+    diagonal = source[:, 0:HD] == lane[:, 0:HD]
+    unused = jnp.zeros((1, HD), F32)
     found = jnp.zeros((64, 256), F32)
     holders = []
     for i in range(3):
         key = keys[:, i : i + 1]
         found = found + jnp.where(key == target, tile + float(i), 0.0)
         request = jnp.floor(jnp.maximum(key, 0.0) * 0.25)
-        holders.append(jnp.sum(jnp.where(diagonal, request, 0.0), axis=0, keepdims=True))
+        holder = jnp.sum(jnp.where(diagonal, request, 0.0), axis=0, keepdims=True)
+        holders.append(jnp.concatenate([holder, unused], axis=1))
     found = jnp.minimum(jnp.sum(found, axis=0, keepdims=True), 255.0)
     table[...] = jnp.concatenate([found] + holders, axis=0).astype(jnp.int32)
     copy = pltpu.make_async_copy(table, table_s, sem)

time: 107 us -> 107 us (level)
  no operation moved by 1% of the time
where the time goes in v7:
time: 107 us
  blocking collectives  37.7 us (35%)
  starting transfers between devices  32.9 us (31%)
  waiting for transfers between devices  25.9 us (24%)
  Pallas kernels  9.34 us (9%)
    all_to_all x1, blocking collectives, shards(): partials = to_all(partial, 'tp')  20.2 us
    all_to_all x1, blocking collectives, shards(): gathered = near(to_all(attention, 'req', axis_index_groups=spot))  17.5 us
    all_to_all x1, starting transfers between devices, shards(): pieces = to_all(packed, 'req')  10.9 us
    ppermute x1, waiting for transfers between devices, shards(): place_rows = lax.ppermute(own_rows, 'req', moves)  8.6 us
    all_to_all x1, starting transfers between devices, shards(): home = to_all(routed, 'req')  6.9 us
    ppermute x3, starting transfers between devices, swap(): lax.ppermute(x, 'req', [(spot[a][b], spot[a ^ flip][b]) for a in range(8)...  6.73 us
    ppermute x3, waiting for transfers between devices, swap(): lax.ppermute(x, 'req', [(spot[a][b], spot[a ^ flip][b]) for a in range(8)...  6.16 us
    all_to_all x1, waiting for transfers between devices, shards(): pieces = to_all(packed, 'req')  5.93 us
  transfers between devices with their start and end apart: 7, of which 6 were waited for; matrix products, arithmetic and copies ran while one was open for 0% of the time, Pallas kernels for 2%

profile of v7, /device:TPU:6, one launch (start us, length us, event | category | flops | bytes accessed | tf_op | source)
XLA Modules:
  0.0 106.7 jit_solution(822124525862077001)
XLA Ops:
  0.6 2.0 %pack.1 = (bf16[64,4,8,128]{3,2,1,0:T(8,128)(2,1)}, bf16[32,768]{1,0:T(8,128)(2,1)}) custom-call(s32[2,3]{1,0:T(2,128)} %bitcast.11, s32[8,64]{1,0:T(8,128)} %bitcast.9, bf16[3,256,256]{2,1,0:T(8,128)(2,1)} %cache.3, bf16[1,28,512]{2,1,0:T(8,128)(2,1)} %query.1, bf16[1,28,256]{2,1,0:T(8,128)(2,1)} %tree.1, s32[1,28]{1,0:T(1,128)} %parent.1), custom_call_target="tpu_custom_call" | custom-call | tf_op jit(solution)/shard_map/spread/pack/pallas_call | solution.py:245
  2.7 0.0 copy-start
  2.7 10.9 %all-to-all-start = ((bf16[64,4,8,128]{3,2,1,0:T(8,128)(2,1)}), bf16[64,4,8,128]{3,2,1,0:T(8,128)(2,1)S(1)}, u32[]{:S(2)}, u32[]{:S(2)}) async-start(bf16[64,4,8,128]{3,2,1,0:T(8,128)(2,1)} %get-tuple-element.13), calls=%async_computation | async-start | bytes 1048576 | tf_op jit(solution)/shard_map/spread/all_to_all | solution.py:252
  13.6 0.0 copy-done
  13.6 2.7 %collective-permute-start = (bf16[1,64,512]{2,1,0:T(8,128)(2,1)S(1)}, bf16[1,64,512]{2,1,0:T(8,128)(2,1)S(1)}, u32[]{:S(2)}, u32[]{:S(2)}) collective-permute-start(bf16[1,64,512]{2,1,0:T(8,128)(2,1)S(1)} %bitcast.6), channel_id=1, source_target_pairs={{0,128},{16,144},{32,160},{48,176},{64,192},{80,208},{96,224},{112... | collective-permute-start | bytes 196616 | tf_op jit(solution)/shard_map/weight_gather/ppermute | solution.py:236
  16.3 4.8 %collective-permute-done = bf16[1,64,512]{2,1,0:T(8,128)(2,1)S(1)} collective-permute-done((bf16[1,64,512]{2,1,0:T(8,128)(2,1)S(1)}, bf16[1,64,512]{2,1,0:T(8,128)(2,1)S(1)}, u32[]{:S(2)}, u32[]{:S(2)}) %collective-permute-start) | collective-permute-done | bytes 65568 | tf_op jit(solution)/shard_map/weight_gather/ppermute | solution.py:236
  21.1 1.9 %collective-permute-start.1 = (bf16[2,64,512]{2,1,0:T(8,128)(2,1)S(1)}, bf16[2,64,512]{2,1,0:T(8,128)(2,1)S(1)}, u32[]{:S(2)}, u32[]{:S(2)}) collective-permute-start(bf16[2,64,512]{2,1,0:T(8,128)(2,1)S(1)} %pad_maximum_fusion), channel_id=1, source_target_pairs={{0,8},{16,24},{32,40},{48,56},{64,72},{80,88},{96,104},{112,120},{... | collective-permute-start | bytes 393224 | tf_op jit(solution)/shard_map/weight_gather/ppermute | solution.py:236
  23.1 1.3 %collective-permute-done.1 = bf16[2,64,512]{2,1,0:T(8,128)(2,1)S(1)} collective-permute-done((bf16[2,64,512]{2,1,0:T(8,128)(2,1)S(1)}, bf16[2,64,512]{2,1,0:T(8,128)(2,1)S(1)}, u32[]{:S(2)}, u32[]{:S(2)}) %collective-permute-start.1) | collective-permute-done | bytes 131104 | tf_op jit(solution)/shard_map/weight_gather/ppermute | solution.py:236
  24.4 5.9 %all-to-all-done.got = bf16[64,4,8,128]{3,2,1,0:T(8,128)(2,1)S(1)} async-done(((bf16[64,4,8,128]{3,2,1,0:T(8,128)(2,1)}), bf16[64,4,8,128]{3,2,1,0:T(8,128)(2,1)S(1)}, u32[]{:S(2)}, u32[]{:S(2)}) %all-to-all-start) | async-done | bytes 524320 | tf_op jit(solution)/shard_map/spread/all_to_all | solution.py:252
  30.3 2.2 %route.1 = (bf16[64,4,8,128]{3,2,1,0:T(8,128)(2,1)}, bf16[8,8,128]{2,1,0:T(8,128)(2,1)S(1)}) custom-call(bf16[64,4,8,128]{3,2,1,0:T(8,128)(2,1)S(1)} %all-to-all-done.got), custom_call_target="tpu_custom_call" | custom-call | tf_op jit(solution)/shard_map/route/route/pallas_call | solution.py:255
  32.5 6.9 %all-to-all-start.1 = ((bf16[64,4,8,128]{3,2,1,0:T(8,128)(2,1)}), bf16[64,4,8,128]{3,2,1,0:T(8,128)(2,1)S(1)}, u32[]{:S(2)}, u32[]{:S(2)}) async-start(bf16[64,4,8,128]{3,2,1,0:T(8,128)(2,1)} %get-tuple-element.16), calls=%async_computation.1 | async-start | bytes 1048576 | tf_op jit(solution)/shard_map/route/all_to_all | solution.py:269
  39.4 0.0 copy-start.1
  39.5 2.2 %collective-permute-start.2 = (bf16[4,64,512]{2,1,0:T(8,128)(2,1)S(1)}, bf16[4,64,512]{2,1,0:T(8,128)(2,1)S(1)}, u32[]{:S(2)}, u32[]{:S(2)}) collective-permute-start(bf16[4,64,512]{2,1,0:T(8,128)(2,1)S(1)} %constant_dynamic-update-slice_fusion.first_weight), channel_id=1, source_target_pairs={{0,384},{16,400},{32,416},{48,432},{64,448},{80,464},{96,480},{112... | collective-permute-start | bytes 786440 | tf_op jit(solution)/shard_map/route/ppermute | solution.py:236
  41.6 0.0 copy-done.1
  41.6 5.4 %collective-permute-start.3 = (bf16[32,768]{1,0:T(8,128)(2,1)S(1)}, bf16[32,768]{1,0:T(8,128)(2,1)S(1)}, u32[]{:S(2)}, u32[]{:S(2)}) collective-permute-start(bf16[32,768]{1,0:T(8,128)(2,1)S(1)} %copy-done.1), channel_id=1, source_target_pairs={{0,96},{8,112},{16,0},{24,16},{32,32},{40,48},{48,64},{56,80},{64,... | collective-permute-start | bytes 147464 | tf_op jit(solution)/shard_map/route/ppermute | solution.py:273
  47.1 8.6 %collective-permute-done.3.own_rows = bf16[32,768]{1,0:T(8,128)(2,1)S(1)} collective-permute-done((bf16[32,768]{1,0:T(8,128)(2,1)S(1)}, bf16[32,768]{1,0:T(8,128)(2,1)S(1)}, u32[]{:S(2)}, u32[]{:S(2)}) %collective-permute-start.3) | collective-permute-done | bytes 49184 | tf_op jit(solution)/shard_map/route/ppermute | solution.py:273
  55.7 0.0 collective-permute-done.2.last_weight
  55.7 0.5 all-to-all-done.1.got
  56.1 1.9 %attend.1 = bf16[8,136,128]{2,1,0:T(8,128)(2,1)S(1)} custom-call(s32[64]{0:T(128)} %lens.3, bf16[32,768]{1,0:T(8,128)(2,1)S(1)} %collective-permute-done.3.own_rows, bf16[64,4,8,128]{3,2,1,0:T(8,128)(2,1)S(1)} %all-to-all-done.1.got, bf16[8,8,128]{2,1,0:T(8,128)(2,1)S(1)} %get-tuple-element.22.fresh_rows), custom_call_target="tpu_custom_call" | custom-call | tf_op jit(solution)/shard_map/attend/attend/pallas_call | solution.py:276
  58.0 17.5 %all_to_all.20.att.got = bf16[8,136,128]{2,1,0:T(8,128)(2,1)S(1)} all-to-all(bf16[8,136,128]{2,1,0:T(8,128)(2,1)S(1)} %attend.1), channel_id=1, replica_groups={{0,16,32,48,64,80,96,112},{128,144,160,176,192,208,224,240},{256,272,28..., dimensions={0} | all-to-all | bytes 557056 | tf_op jit(solution)/shard_map/attend/all_to_all | solution.py:279
  75.5 0.5 project.1
  76.0 20.2 %all_to_all.21.got = bf16[8,112,128]{2,1,0:T(8,128)(2,1)S(1)} all-to-all(bf16[8,112,128]{2,1,0:T(8,128)(2,1)S(1)} %project.1), channel_id=1, replica_groups=mesh['req'=64,'tp'=8] {'tp'}, dimensions={0} | all-to-all | bytes 458752 | tf_op jit(solution)/shard_map/project/all_to_all | solution.py:292
  96.3 2.9 %collective-permute-start.4 = (bf16[112,128]{1,0:T(8,128)(2,1)S(1)}, bf16[112,128]{1,0:T(8,128)(2,1)S(1)}, u32[]{:S(2)}, u32[]{:S(2)}) collective-permute-start(bf16[112,128]{1,0:T(8,128)(2,1)S(1)} %total.1), channel_id=1, source_target_pairs={{0,0},{1,128},{2,256},{3,384},{4,8},{5,136},{6,264},{7,392},{16,16... | collective-permute-start | bytes 86024 | tf_op jit(solution)/shard_map/project/ppermute | solution.py:295
  99.2 2.0 %append.1 = bf16[3,256,256]{2,1,0:T(8,128)(2,1)} custom-call(s32[2,3]{1,0:T(2,128)} %bitcast.12, s32[64]{0:T(128)} %lens.3, s32[8,64]{1,0:T(8,128)} %bitcast.10, bf16[3,256,256]{2,1,0:T(8,128)(2,1)} %cache.3, bf16[8,136,128]{2,1,0:T(8,128)(2,1)S(1)} %all_to_all.20.att.got), custom_call_target="tpu_custom_call" | custom-call | tf_op jit(solution)/shard_map/append/append/pallas_call | solution.py:281
  101.3 4.7 %collective-permute-done.4.got = bf16[112,128]{1,0:T(8,128)(2,1)S(1)} collective-permute-done((bf16[112,128]{1,0:T(8,128)(2,1)S(1)}, bf16[112,128]{1,0:T(8,128)(2,1)S(1)}, u32[]{:S(2)}, u32[]{:S(2)}) %collective-permute-start.4) | collective-permute-done | bytes 28704 | tf_op jit(solution)/shard_map/project/ppermute | solution.py:295
  106.0 0.7 place.1
  (4 shorter events, 0.1 us)
Async XLA Ops:
  2.7 10.9 %copy-start = (bf16[512,64]{0,1:T(8,128)(2,1)S(1)}, bf16[512,64]{0,1:T(8,128)(2,1)}, u32[]{:S(2)}) copy-start(bf16[512,64]{0,1:T(8,128)(2,1)} %param.15) | copy-start | bytes 196612
  2.7 27.7 %all-to-all-start = ((bf16[64,4,8,128]{3,2,1,0:T(8,128)(2,1)}), bf16[64,4,8,128]{3,2,1,0:T(8,128)(2,1)S(1)}, u32[]{:S(2)}, u32[]{:S(2)}) async-start(bf16[64,4,8,128]{3,2,1,0:T(8,128)(2,1)} %get-tuple-element.13), calls=%async_computation | async-start | bytes 1048576 | tf_op jit(solution)/shard_map/spread/all_to_all | solution.py:252
  13.6 7.5 %collective-permute-start = (bf16[1,64,512]{2,1,0:T(8,128)(2,1)S(1)}, bf16[1,64,512]{2,1,0:T(8,128)(2,1)S(1)}, u32[]{:S(2)}, u32[]{:S(2)}) collective-permute-start(bf16[1,64,512]{2,1,0:T(8,128)(2,1)S(1)} %bitcast.6), channel_id=1, source_target_pairs={{0,128},{16,144},{32,160},{48,176},{64,192},{80,208},{96,224},{112... | collective-permute-start | bytes 196616 | tf_op jit(solution)/shard_map/weight_gather/ppermute | solution.py:236
  21.1 3.2 %collective-permute-start.1 = (bf16[2,64,512]{2,1,0:T(8,128)(2,1)S(1)}, bf16[2,64,512]{2,1,0:T(8,128)(2,1)S(1)}, u32[]{:S(2)}, u32[]{:S(2)}) collective-permute-start(bf16[2,64,512]{2,1,0:T(8,128)(2,1)S(1)} %pad_maximum_fusion), channel_id=1, source_target_pairs={{0,8},{16,24},{32,40},{48,56},{64,72},{80,88},{96,104},{112,120},{... | collective-permute-start | bytes 393224 | tf_op jit(solution)/shard_map/weight_gather/ppermute | solution.py:236
  32.5 23.6 %all-to-all-start.1 = ((bf16[64,4,8,128]{3,2,1,0:T(8,128)(2,1)}), bf16[64,4,8,128]{3,2,1,0:T(8,128)(2,1)S(1)}, u32[]{:S(2)}, u32[]{:S(2)}) async-start(bf16[64,4,8,128]{3,2,1,0:T(8,128)(2,1)} %get-tuple-element.16), calls=%async_computation.1 | async-start | bytes 1048576 | tf_op jit(solution)/shard_map/route/all_to_all | solution.py:269
  39.4 2.2 %copy-start.1 = (bf16[32,768]{1,0:T(8,128)(2,1)S(1)}, bf16[32,768]{1,0:T(8,128)(2,1)}, u32[]{:S(2)}) copy-start(bf16[32,768]{1,0:T(8,128)(2,1)} %get-tuple-element.19) | copy-start | bytes 147460
  39.5 16.2 %collective-permute-start.2 = (bf16[4,64,512]{2,1,0:T(8,128)(2,1)S(1)}, bf16[4,64,512]{2,1,0:T(8,128)(2,1)S(1)}, u32[]{:S(2)}, u32[]{:S(2)}) collective-permute-start(bf16[4,64,512]{2,1,0:T(8,128)(2,1)S(1)} %constant_dynamic-update-slice_fusion.first_weight), channel_id=1, source_target_pairs={{0,384},{16,400},{32,416},{48,432},{64,448},{80,464},{96,480},{112... | collective-permute-start | bytes 786440 | tf_op jit(solution)/shard_map/route/ppermute | solution.py:236
  41.6 14.0 %collective-permute-start.3 = (bf16[32,768]{1,0:T(8,128)(2,1)S(1)}, bf16[32,768]{1,0:T(8,128)(2,1)S(1)}, u32[]{:S(2)}, u32[]{:S(2)}) collective-permute-start(bf16[32,768]{1,0:T(8,128)(2,1)S(1)} %copy-done.1), channel_id=1, source_target_pairs={{0,96},{8,112},{16,0},{24,16},{32,32},{40,48},{48,64},{56,80},{64,... | collective-permute-start | bytes 147464 | tf_op jit(solution)/shard_map/route/ppermute | solution.py:273
  96.3 9.7 %collective-permute-start.4 = (bf16[112,128]{1,0:T(8,128)(2,1)S(1)}, bf16[112,128]{1,0:T(8,128)(2,1)S(1)}, u32[]{:S(2)}, u32[]{:S(2)}) collective-permute-start(bf16[112,128]{1,0:T(8,128)(2,1)S(1)} %total.1), channel_id=1, source_target_pairs={{0,0},{1,128},{2,256},{3,384},{4,8},{5,136},{6,264},{7,392},{16,16... | collective-permute-start | bytes 86024 | tf_op jit(solution)/shard_map/project/ppermute | solution.py:295
